TPU v7x, 256 devices: a whole 4x4x8 slice. The times are simulated.
256 devices in a mesh: dp: 32 (over y, x, z_lo), mp: 8 (over z_hi, core).
Axes of the slice: x: 4, y: 4, z: 8 (z_hi: 4, z_lo: 2; z = z_hi * 2 + z_lo), core: 2. Of those that a mesh axis runs over, the one named last changes fastest.
Arguments:
- inputs: bfloat16 [4096, 16384], P('dp', 'mp'), may hold values from -6 to 6
- projector: bfloat16 [16384, 1024], P('dp', 'mp'), may hold values from -0.046875 to 0.046875
- out_grads: bfloat16 [4096, 26624], P('dp', 'mp'), may hold values from -0.25 to 0.25
- weights: bfloat16 [16384, 26624], P('dp', 'mp'), may hold values from -6 to 6
- first_moment: float32 [1024, 26624], P('dp', 'mp'), may hold values from -1.5 to 1.5
- second_moment: float32 [1024, 26624], P('dp', 'mp'), may hold values from 0.01 to 1
Outputs:
- new_weights: bfloat16 [16384, 26624], P('dp', 'mp')
- new_first: float32 [1024, 26624], P('dp', 'mp')
- new_second: float32 [1024, 26624], P('dp', 'mp')
All inputs are finite; a program needn't handle non-finite values.
Results may differ from a plain program's by a relative error of at most 0.0031.
Values may be sent and summed in bfloat16 or wider, within the bound.
A program may use at most 128 MiB of HBM per device.

v0:
```python
import jax
import jax.numpy as jnp
from jax import lax
from jax.sharding import Mesh
from jax.sharding import PartitionSpec as P

STEP = 1000
DP = ("dp_0", "dp_1", "dp_2")
MP = ("mp_0", "mp_1")


def joined_along(parts, dim):
    dims = list(parts.shape[1:])
    dims[dim] *= parts.shape[0]
    return jnp.moveaxis(parts, 0, dim).reshape(dims)


def copy_for_each(x, axis):
    peers = lax.axis_size(axis)
    return lax.all_to_all(jnp.broadcast_to(x[None], (peers, *x.shape)), axis, 0, 0, tiled=True)


def collect(x, axis, dim):
    return joined_along(copy_for_each(x, axis), dim)


def summed_rows(total, axes):
    for axis in axes:
        total = lax.psum_scatter(total, axis, scatter_dimension=0, tiled=True)
    return total


def stacked_from(x, axes, order):
    parts = x[None]
    for k in order:
        parts = lax.all_gather(parts, axes[k], axis=0, tiled=True)
    block = [lax.axis_size(axes[k]) for k in reversed(order)]
    parts = parts.reshape(*block, *x.shape)
    turned = sorted(range(len(order)), key=lambda place: order[len(order) - 1 - place])
    return parts.transpose(*turned, *range(len(order), parts.ndim)).reshape(-1, *x.shape)


def gather_axes(x, axes, order, dim):
    return joined_along(stacked_from(x, axes, order), dim)


def per_device(inputs, projector, out_grads, weights, first_moment, second_moment):
    columns = collect(projector, DP, 0)
    own_part = jnp.dot(
        lax.all_gather(inputs, MP, axis=1, tiled=True), columns, preferred_element_type=jnp.float32
    )
    projected = collect(own_part.astype(jnp.bfloat16), MP, 1)
    compressed = summed_rows(
        lax.dot_general(
            projected, out_grads, (((0,), (0,)), ((), ())), preferred_element_type=jnp.float32
        ),
        DP,
    )
    new_first = 0.9 * first_moment + 0.1 * compressed
    new_second = 0.999 * second_moment + 0.001 * compressed * compressed
    first_fix = 1.0 - 0.9**STEP
    second_fix = 1.0 - 0.999**STEP
    direction = (new_first / first_fix / (jnp.sqrt(new_second / second_fix) + 1e-08)).astype(
        jnp.bfloat16
    )
    full_rows = gather_axes(projector, MP, (0, 1), 1)
    empty = jnp.zeros(weights.shape, jnp.float32)
    piece = lax.all_gather(direction, DP, axis=0, tiled=True)
    ranks = lax.slice_in_dim(full_rows, 0, piece.shape[0], axis=1)
    lifted = empty + jnp.dot(ranks, piece, preferred_element_type=jnp.float32)
    new_weights = (weights.astype(jnp.float32) - 2.0 * lifted).astype(jnp.bfloat16)
    return (new_weights, new_first, new_second)


def solution(mesh):
    finer = Mesh(mesh.devices.reshape(4, 4, 2, 4, 2), ("dp_0", "dp_1", "dp_2", "mp_0", "mp_1"))
    in_specs = (P(DP, MP), P(DP, MP), P(DP, MP), P(DP, MP), P(DP, MP), P(DP, MP))
    out_specs = (P(DP, MP), P(DP, MP), P(DP, MP))
    return jax.shard_map(
        per_device, mesh=finer, in_specs=in_specs, out_specs=out_specs, check_vma=False
    )
```

profile of v0, /device:TPU:4, one launch (start us, length us, event | category | flops | bytes accessed | tf_op | source)
XLA Modules:
  0.0 528.1 jit_solution(4391776235239729843)
XLA Ops:
  8.0 0.0 copy-start
  8.0 3.9 broadcast_in_dim.6
  11.9 9.0 %all-to-all-start = ((bf16[32,512,128]{2,1,0:T(8,128)(2,1)}), bf16[32,512,128]{2,1,0:T(8,128)(2,1)}, u32[]{:S(2)}, u32[]{:S(2)}) async-start(bf16[32,512,128]{2,1,0:T(8,128)(2,1)} %broadcast_in_dim.6), calls=%async_computation | async-start | bytes 8388608 | tf_op jit(solution)/shard_map/all_to_all | solution.py:20
  20.9 0.0 all-gather.5.cloned.1.call-start
  21.0 0.7 all-gather.5.cloned.1.call-update
  21.7 0.0 reduce-scatter.4.cloned.1.call-start
  21.7 73.5 %all-gather.5.cloned.1.call-done = bf16[128,16384]{1,0:T(8,128)(2,1)} async-done(((bf16[128,2048]{1,0:T(8,128)(2,1)}), bf16[128,16384]{1,0:T(8,128)(2,1)}) %all-gather.5.cloned.1.call-update) | async-done | bytes 4194320 | tf_op jit(solution)/shard_map/all_gather | solution.py:50
  95.2 6.6 %all-to-all-done = bf16[32,512,128]{2,1,0:T(8,128)(2,1)} async-done(((bf16[32,512,128]{2,1,0:T(8,128)(2,1)}), bf16[32,512,128]{2,1,0:T(8,128)(2,1)}, u32[]{:S(2)}, u32[]{:S(2)}) %all-to-all-start) | async-done | bytes 4194336 | tf_op jit(solution)/shard_map/all_to_all | solution.py:20
  101.8 4.7 convolution_convert_fusion
  106.5 0.1 copy.21
  106.7 19.9 %all_to_all.10 = bf16[8,128,128]{1,2,0:T(8,128)(2,1)S(1)} all-to-all(bf16[8,128,128]{1,2,0:T(8,128)(2,1)S(1)} %broadcast_in_dim.7), channel_id=1, replica_groups=mesh['dp_0'=4,'dp_1'=4,'dp_2'=2,'mp_0'=4,'mp_1'=2] {'mp_0','mp_1'}, dimensions={0} | all-to-all | bytes 524288 | tf_op jit(solution)/shard_map/all_to_all | solution.py:20
  126.6 6.8 %fusion.3 = f32[1024,3328]{1,0:T(8,128)} fusion(bf16[128,1024]{0,1:T(8,128)(2,1)S(1)} %bitcast.24, bf16[128,3328]{1,0:T(8,128)(2,1)S(1)} %copy-done), kind=kOutput, calls=%fused_computation.7 | convolution fusion | flops 872415232 | bytes 14745600 | tf_op jit(solution)/shard_map/dot_general | solution.py:54
  133.5 0.0 reduce-scatter.4.cloned.1.call-update
  133.5 0.0 reduce-scatter.6.cloned.1.call-start
  133.6 122.2 %reduce-scatter.4.cloned.1.call-done = f32[256,3328]{1,0:T(8,128)} async-done(((f32[1024,3328]{1,0:T(8,128)}), f32[256,3328]{1,0:T(8,128)}) %reduce-scatter.4.cloned.1.call-update) | async-done | bytes 3407888 | tf_op jit(solution)/shard_map/reduce_scatter | solution.py:29
  255.7 0.0 reduce-scatter.6.cloned.1.call-update
  255.7 0.0 reduce-scatter.8.cloned.1.call-start
  255.8 43.7 %reduce-scatter.6.cloned.1.call-done = f32[64,3328]{1,0:T(8,128)} async-done(((f32[256,3328]{1,0:T(8,128)}), f32[64,3328]{1,0:T(8,128)}) %reduce-scatter.6.cloned.1.call-update) | async-done | bytes 851984 | tf_op jit(solution)/shard_map/reduce_scatter | solution.py:29
  299.5 0.0 reduce-scatter.8.cloned.1.call-update
  299.5 0.0 all-gather.9.cloned.1.call-start
  299.6 20.2 %all-gather = bf16[2048,128]{1,0:T(8,128)(2,1)} all-gather(bf16[512,128]{1,0:T(8,128)(2,1)S(1)} %copy-done.1), channel_id=2, replica_groups=mesh['dp_0'=4,'dp_1'=4,'dp_2'=2,'mp_0'=4,'mp_1'=2] {'mp_0'}, dimensions={0}, use_global_device_ids=true | all-gather | bytes 655360 | tf_op jit(solution)/shard_map/all_gather | solution.py:36
  319.8 0.0 all-gather.9.cloned.1.call-update
  319.8 0.0 all-gather.7.cloned.1.call-start
  319.9 7.4 %reduce-scatter.8.cloned.1.call-done = f32[32,3328]{1,0:T(8,128)} async-done(((f32[64,3328]{1,0:T(8,128)}), f32[32,3328]{1,0:T(8,128)}) %reduce-scatter.8.cloned.1.call-update) | async-done | bytes 426000 | tf_op jit(solution)/shard_map/reduce_scatter | solution.py:29
  327.3 2.1 divide_convert_fusion
  329.4 0.0 all-gather.7.cloned.1.call-update
  329.4 5.6 %copy.20 = bf16[512,3328]{0,1:T(8,128)(2,1)} copy(bf16[512,3328]{1,0:T(8,128)(2,1)} %param.9) | data formatting | bytes 6815744 | tf_op args[3]
  335.0 1.3 copy.22
  336.3 0.5 copy.23
  336.9 169.8 %all-gather.7.cloned.1.call-done = bf16[1024,3328]{1,0:T(8,128)(2,1)} async-done(((bf16[32,3328]{1,0:T(8,128)(2,1)}), bf16[1024,3328]{1,0:T(8,128)(2,1)}) %all-gather.7.cloned.1.call-update) | async-done | bytes 6815760 | tf_op jit(solution)/shard_map/all_gather | solution.py:68
  506.7 8.7 %fusion = bf16[512,3328]{0,1:T(8,128)(2,1)} fusion(bf16[512,3328]{0,1:T(8,128)(2,1)} %copy.20, bf16[1024,3328]{1,0:T(8,128)(2,1)} %all-gather.7.cloned.1.call-done, bf16[512,1024]{0,1:T(8,128)(2,1)S(1)} %bitcast.26), kind=kOutput, calls=%fused_computation.1 | convolution fusion | flops 3496476672 | bytes 14680064 | tf_op jit(solution)/shard_map/dot_general | solution.py:70
  515.4 5.5 %copy.24 = bf16[512,3328]{1,0:T(8,128)(2,1)} copy(bf16[512,3328]{0,1:T(8,128)(2,1)} %fusion) | data formatting | bytes 6815744
  (9 shorter events, 0.1 us)
Async XLA Ops:
  8.0 118.6 %copy-start = (bf16[128,3328]{1,0:T(8,128)(2,1)S(1)}, bf16[128,3328]{1,0:T(8,128)(2,1)}, u32[]{:S(2)}) copy-start(bf16[128,3328]{1,0:T(8,128)(2,1)} %param.8) | copy-start | bytes 2555908
  11.9 89.9 %all-to-all-start = ((bf16[32,512,128]{2,1,0:T(8,128)(2,1)}), bf16[32,512,128]{2,1,0:T(8,128)(2,1)}, u32[]{:S(2)}, u32[]{:S(2)}) async-start(bf16[32,512,128]{2,1,0:T(8,128)(2,1)} %broadcast_in_dim.6), calls=%async_computation | async-start | bytes 8388608 | tf_op jit(solution)/shard_map/all_to_all | solution.py:20
  20.9 74.3 %all-gather.5.cloned.1.call-start = ((), (), s32[]{:S(2)}) async-start(), calls=%async_computation.5 | async-start | bytes 4718592 | tf_op jit(solution)/shard_map/all_gather | solution.py:50
  21.7 234.1 %reduce-scatter.4.cloned.1.call-start = ((), (), s32[]{:S(2)}) async-start(), calls=%async_computation.6 | async-start | bytes 17039360 | tf_op jit(solution)/shard_map/reduce_scatter | solution.py:29
  133.5 166.1 %copy-start.1 = (bf16[512,128]{1,0:T(8,128)(2,1)S(1)}, bf16[512,128]{1,0:T(8,128)(2,1)}, u32[]{:S(2)}) copy-start(bf16[512,128]{1,0:T(8,128)(2,1)} %param.7) | copy-start | bytes 393220
  133.5 193.8 %copy-start.2 = (f32[32,3328]{1,0:T(8,128)S(1)}, f32[32,3328]{1,0:T(8,128)}, u32[]{:S(2)}) copy-start(f32[32,3328]{1,0:T(8,128)} %param.11) | copy-start | bytes 1277956
  133.5 193.8 %copy-start.3 = (f32[32,3328]{1,0:T(8,128)S(1)}, f32[32,3328]{1,0:T(8,128)}, u32[]{:S(2)}) copy-start(f32[32,3328]{1,0:T(8,128)} %param.10) | copy-start | bytes 1277956
  133.5 166.0 %reduce-scatter.6.cloned.1.call-start = ((), (), s32[]{:S(2)}) async-start(), calls=%async_computation.7 | async-start | bytes 4259840 | tf_op jit(solution)/shard_map/reduce_scatter | solution.py:29
  255.7 71.5 %reduce-scatter.8.cloned.1.call-start = ((), (), s32[]{:S(2)}) async-start(), calls=%async_computation.8 | async-start | bytes 1277952 | tf_op jit(solution)/shard_map/reduce_scatter | solution.py:29
  299.5 35.5 %all-gather.9.cloned.1.call-start = ((), (), s32[]{:S(2)}) async-start(), calls=%async_computation.10 | async-start | bytes 1572864 | tf_op jit(solution)/shard_map/all_gather | solution.py:36
  319.8 186.9 %all-gather.7.cloned.1.call-start = ((), (), s32[]{:S(2)}) async-start(), calls=%async_computation.9 | async-start | bytes 7028736 | tf_op jit(solution)/shard_map/all_gather | solution.py:68
Sparse Core Ops, SparseCore 0:
  23.6 71.6 all-gather.4
  133.6 122.0 reduce-scatter.3
  258.3 41.1 reduce-scatter.5
  301.9 25.3 reduce-scatter.7
Sparse Core Ops, SparseCore 1:
  319.9 13.1 all-gather.8
  334.7 171.9 all-gather.6
where the time goes:
time: 535 us; the launch traced here: 528 us
  waiting for transfers between devices  424 us (79%)
  blocking collectives  40.1 us (7%)
  matrix products  20.3 us (4%)
  local copies, waits for them, and re-layouts  17.1 us (3%)
  between operations  15.3 us (3%)
  starting transfers between devices  9.25 us (2%)
    reduce_scatter x3, waiting for transfers between devices, summed_rows(): total = lax.psum_scatter(total, axis, scatter_dimension=0, tiled=True)  173 us
    all_gather x1, waiting for transfers between devices, per_device(): piece = lax.all_gather(direction, DP, axis=0, tiled=True)  170 us
    all_gather x1, waiting for transfers between devices, per_device(): lax.all_gather(inputs, MP, axis=1, tiled=True)  73.5 us
    all_gather x1, blocking collectives, stacked_from(): parts = lax.all_gather(parts, axes[k], axis=0, tiled=True)  20.2 us
    all_to_all x1, blocking collectives, copy_for_each(): lax.all_to_all(jnp.broadcast_to(x[None], (peers, *x.shape)), axis, 0, 0,...  19.9 us
    unnamed x10, local copies, waits for them, and re-layouts  11.2 us
  transfers between devices with their start and end apart: 7, of which 6 were waited for; matrix products, arithmetic and copies ran while one was open for 2% of the time, Pallas kernels for 0%

commit v1 on v0

v1 whole, which is shorter than its diff:
```python
import jax
import jax.numpy as jnp
from jax import lax
from jax.experimental import pallas as pl
from jax.experimental.pallas import tpu as pltpu
from jax.sharding import Mesh
from jax.sharding import PartitionSpec as P

STEP = 1000
AXES = ("dp_0", "dp_1", "dp_2", "mp_0", "mp_1")
DP = AXES[:3]
MP = AXES[3:]
MESH = pl.DeviceIdType.MESH
ANY = pl.BlockSpec(memory_space=pl.ANY)
VMEM = pl.BlockSpec(memory_space=pltpu.VMEM)
DMA = pltpu.SemaphoreType.DMA


def place():
    return tuple(lax.axis_index(a) for a in AXES)


def remote(src, dst, send_sem, recv_sem, **where):
    return pltpu.make_async_remote_copy(
        src_ref=src,
        dst_ref=dst,
        send_sem=send_sem,
        recv_sem=recv_sem,
        device_id=where,
        device_id_type=MESH,
    )


def landed(dst, sem):
    pltpu.make_async_copy(dst, dst, sem).wait()


def rows(start, size, unit=None):
    return pl.ds(pl.multiple_of(start, unit or size), size)


def greet(peers, extra=None):
    barrier = pltpu.get_barrier_semaphore()
    for peer in peers:
        pl.semaphore_signal(barrier, inc=1, device_id=peer, device_id_type=MESH)
    count = len(peers)
    if extra is not None:
        peer, present = extra

        @pl.when(present)
        def _():
            pl.semaphore_signal(barrier, inc=1, device_id=peer, device_id_type=MESH)

        count = count + present.astype(jnp.int32)
    pl.semaphore_wait(barrier, count)


def projected_kernel(
    inp, proj, grads, pa, g4,
    inp4, pt, pq, part, half_in, rs_in, g_own,
    loc_sem, inp_s, inp_r, g_s, g_r, pt_s, pt_r, pq_s, pq_r, half_s, half_r, rs_s, rs_r, pa_s, pa_r,
):
    y, x, zl, h, c = place()
    up, down = lax.rem(y + 1, 4), lax.rem(y + 3, 4)
    tok = inp.shape[0]
    half = tok // 2
    feat = proj.shape[0]
    lanes = proj.shape[1]
    peers = [{"dp_0": up}, {"dp_0": down}]
    for dx in range(4):
        for dz in range(2):
            for dc in range(2):
                if dx or dz or dc:
                    peers.append({
                        "dp_1": lax.rem(x + dx, 4),
                        "dp_2": lax.rem(zl + dz, 2),
                        "mp_1": lax.rem(c + dc, 2),
                    })
    for dh in range(1, 4):
        for dc in range(2):
            peers.append({"mp_0": lax.rem(h + dh, 4), "mp_1": lax.rem(c + dc, 2)})
    greet(peers, ({"dp_0": h, "mp_0": y}, y != h))

    in_up = remote(inp, inp4.at[1], inp_s.at[0], inp_r.at[0], dp_0=up)
    in_dn = remote(inp, inp4.at[3], inp_s.at[1], inp_r.at[1], dp_0=down)
    swap = remote(proj, pt, pt_s.at[0], pt_r.at[0], dp_0=h, mp_0=y)
    swap_here = pltpu.make_async_copy(proj, pt, pt_r.at[0])

    @pl.when(y != h)
    def _():
        swap.start()

    @pl.when(y == h)
    def _():
        swap_here.start()

    in_up.start()
    in_dn.start()
    own_in = pltpu.make_async_copy(inp, inp4.at[0], loc_sem.at[0])
    own_in.start()
    own_g = pltpu.make_async_copy(grads, g_own, loc_sem.at[1])
    own_g.start()

    landed(pt, pt_r.at[0])
    core = x // 2
    spot = pq.at[rows((lax.rem(x, 2) * 2 + zl) * feat, feat), rows(c * lanes, lanes)]
    mark = (lax.rem(x, 2) * 2 + zl) * 2 + c
    spread = []
    for dx in (1, 3, 2, 0):
        for dz in (1, 0):
            if dx or dz:
                cp = remote(
                    pt, spot, pq_s.at[dx * 2 + dz], pq_r.at[mark],
                    dp_1=lax.rem(x + dx, 4), dp_2=lax.rem(zl + dz, 2), mp_1=core,
                )
                cp.start()
                spread.append(cp)
    other = remote(pt, spot, pq_s.at[0], pq_r.at[mark], mp_1=1 - c)
    here = pltpu.make_async_copy(pt, spot, pq_r.at[mark])

    @pl.when(core != c)
    def _():
        other.start()

    @pl.when(core == c)
    def _():
        here.start()

    in_up.wait_recv()
    fw_up = remote(
        inp4.at[1, pl.ds(0, half)], inp4.at[2, pl.ds(0, half)], inp_s.at[2], inp_r.at[2], dp_0=up
    )
    fw_up.start()
    in_dn.wait_recv()
    fw_dn = remote(
        inp4.at[3, pl.ds(half, half)], inp4.at[2, pl.ds(half, half)], inp_s.at[3], inp_r.at[3], dp_0=down
    )
    fw_dn.start()
    g_up = remote(grads, g4.at[pl.ds(tok, tok)], g_s.at[0], g_r.at[0], dp_0=up)
    g_dn = remote(grads, g4.at[pl.ds(3 * tok, tok)], g_s.at[1], g_r.at[1], dp_0=down)
    g_up.start()
    g_dn.start()
    own_g.wait()
    put_g = pltpu.make_async_copy(g_own, g4.at[pl.ds(0, tok)], loc_sem.at[2])
    put_g.start()

    own_in.wait()
    for k in range(8):
        landed(pq.at[pl.ds((k // 2) * feat, feat), pl.ds((k % 2) * lanes, lanes)], pq_r.at[k])
    for b in (0, 1, 3):
        part[pl.ds(b * tok, tok)] = jnp.dot(inp4[b], pq[...], preferred_element_type=jnp.float32)
    fw_up.wait_recv()
    fw_dn.wait_recv()
    part[pl.ds(2 * tok, tok)] = jnp.dot(inp4[2], pq[...], preferred_element_type=jnp.float32)

    many = 2 * tok
    pair = remote(part.at[rows((1 - c) * many, many)], half_in, half_s.at[0], half_r.at[0], mp_1=1 - c)
    pair.start()
    pair.wait()
    mine = rows(c * many, many)
    part[mine] += half_in[...]
    cut = many // 4
    sums = []
    for dh in range(1, 4):
        to = lax.rem(h + dh, 4)
        cp = remote(
            part.at[rows(c * many + to * cut, cut)], rs_in.at[dh - 1], rs_s.at[dh - 1], rs_r.at[dh - 1], mp_0=to
        )
        cp.start()
        sums.append(cp)
    for cp in sums:
        cp.wait_recv()
    piece = rows(c * many + h * cut, cut)
    pa[piece] = (part[piece] + rs_in[0] + rs_in[1] + rs_in[2]).astype(pa.dtype)
    shares = []
    for dh in range(4):
        for dc in range(2):
            if dh or dc:
                k = dh * 2 + dc - 1
                cp = remote(
                    pa.at[piece], pa.at[piece], pa_s.at[k], pa_r.at[k],
                    mp_0=lax.rem(h + dh, 4), mp_1=lax.rem(c + dc, 2),
                )
                cp.start()
                shares.append(cp)

    g_up.wait_recv()
    gf_up = remote(
        g4.at[pl.ds(tok, half)], g4.at[pl.ds(2 * tok, half)], g_s.at[2], g_r.at[2], dp_0=up
    )
    gf_up.start()
    g_dn.wait_recv()
    gf_dn = remote(
        g4.at[pl.ds(3 * tok + half, half)], g4.at[pl.ds(2 * tok + half, half)], g_s.at[3], g_r.at[3], dp_0=down
    )
    gf_dn.start()

    for k in range(1, 8):
        frm_h, frm_c = lax.rem(h + 4 - k // 2, 4), lax.rem(c + 2 - k % 2, 2)
        landed(pa.at[rows(frm_c * many + frm_h * cut, cut)], pa_r.at[k - 1])
    gf_up.wait_recv()
    gf_dn.wait_recv()
    put_g.wait()
    for cp in (in_up, in_dn, fw_up, fw_dn, g_up, g_dn, gf_up, gf_dn, *spread, *sums, *shares):
        cp.wait_send()

    @pl.when(y != h)
    def _():
        swap.wait_send()

    @pl.when(core != c)
    def _():
        other.wait_send()


def gather_projected(inputs, projector, out_grads):
    tok, feats = inputs.shape
    feat, lanes = projector.shape
    cols = out_grads.shape[1]
    bf, f32 = jnp.bfloat16, jnp.float32
    return pl.pallas_call(
        projected_kernel,
        name="gather_projected",
        out_shape=(
            jax.ShapeDtypeStruct((4 * tok, 2 * lanes), bf),
            jax.ShapeDtypeStruct((4 * tok, cols), bf),
        ),
        in_specs=[ANY] * 3,
        out_specs=(VMEM, ANY),
        scratch_shapes=[
            pltpu.VMEM((4, tok, feats), bf),
            pltpu.VMEM((feat, lanes), bf),
            pltpu.VMEM((4 * feat, 2 * lanes), bf),
            pltpu.VMEM((4 * tok, 2 * lanes), f32),
            pltpu.VMEM((2 * tok, 2 * lanes), f32),
            pltpu.VMEM((3, tok // 2, 2 * lanes), f32),
            pltpu.VMEM((tok, cols), bf),
            DMA((3,)),
            DMA((4,)), DMA((4,)),
            DMA((4,)), DMA((4,)),
            DMA((1,)), DMA((1,)),
            DMA((8,)), DMA((8,)),
            DMA((1,)), DMA((1,)),
            DMA((3,)), DMA((3,)),
            DMA((7,)), DMA((7,)),
        ],
        compiler_params=pltpu.CompilerParams(collective_id=0, has_side_effects=True),
    )(inputs, projector, out_grads)


def reduce_kernel(
    part, out, raw_l, raw_r, via_l, via_r, turn_r, turn_l, add_l, add_r, zsend, zrecv,
    s_sem, r_sem,
):
    y, x, zl, h, c = place()
    right, left, far = lax.rem(x + 1, 4), lax.rem(x + 3, 4), lax.rem(x + 2, 4)
    n = out.shape[0]
    f32 = jnp.float32
    greet([{"dp_1": right}, {"dp_1": left}, {"dp_2": 1 - zl}])

    def piece(of, half):
        return part.at[rows(of * 2 * n + half * n, n)]

    far_r = remote(piece(far, 0), via_l, s_sem.at[0], r_sem.at[0], dp_1=right)
    far_l = remote(piece(far, 1), via_r, s_sem.at[1], r_sem.at[1], dp_1=left)
    near_r = remote(piece(right, 1), raw_l, s_sem.at[2], r_sem.at[2], dp_1=right)
    near_l = remote(piece(left, 0), raw_r, s_sem.at[3], r_sem.at[3], dp_1=left)
    far_r.start()
    far_l.start()
    near_r.start()
    near_l.start()
    far_r.wait_recv()
    turn_r[...] = (via_l[...].astype(f32) + part[rows(right * 2 * n, n)].astype(f32)).astype(turn_r.dtype)
    on_r = remote(turn_r, add_l, s_sem.at[4], r_sem.at[4], dp_1=right)
    on_r.start()
    far_l.wait_recv()
    turn_l[...] = (via_r[...].astype(f32) + part[rows(left * 2 * n + n, n)].astype(f32)).astype(turn_l.dtype)
    on_l = remote(turn_l, add_r, s_sem.at[5], r_sem.at[5], dp_1=left)
    on_l.start()
    near_r.wait_recv()
    near_l.wait_recv()
    on_r.wait_recv()
    on_l.wait_recv()

    def total(first):
        if first:
            return part[rows(x * 2 * n, n)].astype(f32) + add_l[...].astype(f32) + raw_r[...].astype(f32)
        return part[rows(x * 2 * n + n, n)].astype(f32) + add_r[...].astype(f32) + raw_l[...].astype(f32)

    @pl.when(zl == 0)
    def _():
        zsend[...] = total(False).astype(zsend.dtype)

    @pl.when(zl == 1)
    def _():
        zsend[...] = total(True).astype(zsend.dtype)

    swap = remote(zsend, zrecv, s_sem.at[6], r_sem.at[6], dp_2=1 - zl)
    swap.start()

    @pl.when(zl == 0)
    def _():
        out[...] = total(True)

    @pl.when(zl == 1)
    def _():
        out[...] = total(False)

    swap.wait_recv()
    out[...] += zrecv[...].astype(f32)
    for cp in (far_r, far_l, near_r, near_l, on_r, on_l, swap):
        cp.wait_send()


def reduce_rows(part):
    n, cols = part.shape[0] // 8, part.shape[1]
    slot = pltpu.VMEM((n, cols), part.dtype)
    return pl.pallas_call(
        reduce_kernel,
        name="reduce_rows",
        out_shape=jax.ShapeDtypeStruct((n, cols), jnp.float32),
        in_specs=[VMEM],
        out_specs=VMEM,
        scratch_shapes=[slot] * 10 + [DMA((7,)), DMA((7,))],
        compiler_params=pltpu.CompilerParams(collective_id=1, has_side_effects=True),
    )(part)


def spread_kernel(own, proj, full, prow, stage, loc_sem, z_s, z_r, a_s, a_r, b_s, b_r, p_s, p_r):
    y, x, zl, h, c = place()
    n, cols = own.shape
    lanes = proj.shape[1]
    wide = cols // 2
    rank = (y * 4 + x) * 2 * n
    pair = lax.rem(x + 2, 4)
    peers = [{"dp_2": 1 - zl}]
    for axis, at in (("dp_0", y), ("dp_1", x)):
        peers += [{axis: lax.rem(at + 1, 4)}, {axis: lax.rem(at + 3, 4)}]
    for dh in range(4):
        for dc in range(2):
            if dh or dc:
                if dh == 0:
                    peers.append({"mp_1": 1 - c})
                else:
                    peers.append({"mp_0": lax.rem(h + dh, 4), "mp_1": lax.rem(c + dc, 2)})
    greet(peers)

    mine = full.at[rows(rank + zl * n, n)]
    z = remote(own, mine, z_s, z_r, dp_2=1 - zl)
    z.start()
    put = pltpu.make_async_copy(own, mine, loc_sem.at[0])
    put.start()
    take = pltpu.make_async_copy(proj, stage, loc_sem.at[1])
    take.start()
    put.wait()
    landed(full.at[rows(rank + (1 - zl) * n, n)], z_r)
    take.wait()
    here = prow.at[:, rows((h * 2 + c) * lanes, lanes)]
    keep = pltpu.make_async_copy(stage, here, loc_sem.at[2])
    keep.start()

    sent = []
    todo = []
    colours = []
    for col, s, r, first, second in ((0, a_s, a_r, "dp_1", "dp_0"), (1, b_s, b_r, "dp_0", "dp_1")):
        at1 = x if first == "dp_1" else y
        at2 = y if first == "dp_1" else x
        f1 = 1 if first == "dp_1" else 4
        f2 = 4 if first == "dp_1" else 1

        def region(p1, p2, start, size, col=col, f1=f1, f2=f2):
            return full.at[rows((p1 * f1 + p2 * f2) * 2 * n + start, size, n), pl.ds(col * wide, wide)]

        colours.append((s, r, first, second, at1, at2, region))

    def send(colour, k, axis, to, where):
        s, r = colour[0], colour[1]
        cp = remote(where, where, s.at[k], r.at[k], **{axis: to})
        cp.start()
        sent.append(cp)

    def plus(at, d):
        return lax.rem(at + d, 4)

    for col in colours:
        s, r, first, second, at1, at2, region = col
        send(col, 0, first, plus(at1, 1), region(at1, at2, 0, 2 * n))
        send(col, 1, first, plus(at1, 3), region(at1, at2, 0, 2 * n))
    ahead = []
    for col in colours:
        s, r, first, second, at1, at2, region = col
        landed(region(plus(at1, 3), at2, 0, 2 * n), r.at[0])
        send(col, 2, first, plus(at1, 1), region(plus(at1, 3), at2, 0, n))
        landed(region(plus(at1, 1), at2, 0, 2 * n), r.at[1])
        send(col, 3, first, plus(at1, 3), region(plus(at1, 1), at2, n, n))
    for col in colours:
        s, r, first, second, at1, at2, region = col
        for i, d in enumerate((0, 3, 1)):
            send(col, 4 + i, second, plus(at2, 1), region(plus(at1, d), at2, 0, 2 * n))
            send(col, 8 + i, second, plus(at2, 3), region(plus(at1, d), at2, 0, 2 * n))
    k = 0
    for dh in range(4):
        for dc in range(2):
            if dh or dc:
                where = (
                    {"mp_1": 1 - c} if dh == 0
                    else {"mp_0": lax.rem(h + dh, 4), "mp_1": lax.rem(c + dc, 2)}
                )
                cp = remote(stage, here, p_s.at[k], p_r.at[k], **where)
                cp.start()
                sent.append(cp)
                k += 1
    for col in colours:
        s, r, first, second, at1, at2, region = col
        landed(region(plus(at1, 2), at2, 0, n), r.at[2])
        landed(region(plus(at1, 2), at2, n, n), r.at[3])
        send(col, 7, second, plus(at2, 1), region(plus(at1, 2), at2, 0, 2 * n))
        send(col, 11, second, plus(at2, 3), region(plus(at1, 2), at2, 0, 2 * n))
    for i, d in enumerate((0, 3, 1, 2)):
        for col in colours:
            s, r, first, second, at1, at2, region = col
            landed(region(plus(at1, d), plus(at2, 3), 0, 2 * n), r.at[4 + i])
            send(col, 12 + i, second, plus(at2, 1), region(plus(at1, d), plus(at2, 3), 0, n))
            landed(region(plus(at1, d), plus(at2, 1), 0, 2 * n), r.at[8 + i])
            send(col, 16 + i, second, plus(at2, 3), region(plus(at1, d), plus(at2, 1), n, n))
    for i, d in enumerate((0, 3, 1, 2)):
        for col in colours:
            s, r, first, second, at1, at2, region = col
            landed(region(plus(at1, d), plus(at2, 2), 0, n), r.at[12 + i])
            landed(region(plus(at1, d), plus(at2, 2), n, n), r.at[16 + i])
    k = 0
    for dh in range(4):
        for dc in range(2):
            if dh or dc:
                frm = lax.rem(h + 4 - dh, 4) * 2 + lax.rem(c + 2 - dc, 2)
                landed(prow.at[:, rows(frm * lanes, lanes)], p_r.at[k])
                k += 1
    keep.wait()
    z.wait_send()
    for cp in sent:
        cp.wait_send()


def spread_direction(direction, projector):
    n, cols = direction.shape
    feat, lanes = projector.shape
    bf = jnp.bfloat16
    return pl.pallas_call(
        spread_kernel,
        name="spread_direction",
        out_shape=(
            jax.ShapeDtypeStruct((32 * n, cols), bf),
            jax.ShapeDtypeStruct((feat, 8 * lanes), bf),
        ),
        in_specs=[VMEM, ANY],
        out_specs=(ANY, ANY),
        scratch_shapes=[
            pltpu.VMEM((feat, lanes), bf),
            DMA((3,)),
            DMA, DMA,
            DMA((20,)), DMA((20,)),
            DMA((20,)), DMA((20,)),
            DMA((7,)), DMA((7,)),
        ],
        compiler_params=pltpu.CompilerParams(collective_id=2, has_side_effects=True),
    )(direction, projector)


def per_device(inputs, projector, out_grads, weights, first_moment, second_moment):
    projected, grads = gather_projected(inputs, projector, out_grads)
    part = lax.dot_general(
        projected, grads, (((0,), (0,)), ((), ())), preferred_element_type=jnp.float32
    ).astype(jnp.bfloat16)
    compressed = reduce_rows(part)
    new_first = 0.9 * first_moment + 0.1 * compressed
    new_second = 0.999 * second_moment + 0.001 * compressed * compressed
    first_fix = 1.0 - 0.9**STEP
    second_fix = 1.0 - 0.999**STEP
    direction = (new_first / first_fix / (jnp.sqrt(new_second / second_fix) + 1e-08)).astype(
        jnp.bfloat16
    )
    full, ranks = spread_direction(direction, projector)
    lifted = jnp.dot(ranks, full, preferred_element_type=jnp.float32)
    new_weights = (weights.astype(jnp.float32) - 2.0 * lifted).astype(jnp.bfloat16)
    return (new_weights, new_first, new_second)


def solution(mesh):
    finer = Mesh(mesh.devices.reshape(4, 4, 2, 4, 2), AXES)
    spec = P(DP, MP)
    return jax.shard_map(
        per_device, mesh=finer, in_specs=(spec,) * 6, out_specs=(spec,) * 3, check_vma=False
    )
```

time: 535 us -> 154 us (0.29); the launches traced: 528 us -> 153 us
  waiting for transfers between devices: 424 us -> 0 us
  Pallas kernels: 0 us -> 136 us
  blocking collectives: 40.1 us -> 0 us
  local copies, waits for them, and re-layouts: 17.1 us -> 0.01 us
  between operations: 15.3 us -> 0.69 us
  starting transfers between devices: 9.25 us -> 0 us
  matrix products: 20.3 us -> 14 us
    all_gather x3 -> x0, waiting for transfers between devices: 243 us -> none  [the longest x1 170 us: per_device(): piece = lax.all_gather(direction, DP, axis=0, tiled=True)]
    reduce_scatter x3 -> x0, waiting for transfers between devices: 173 us -> none  [summed_rows(): total = lax.psum_scatter(total, axis, scatter_dimension=0, tiled=True)]
    pallas_call x0 -> x3, Pallas kernels: none -> 136 us  [the longest x1 62.7 us: gather_projected(): pl.pallas_call(projected_kernel, name='gather_projected', out_shape=(jax....]
    all_gather x1 -> x0, blocking collectives: 20.2 us -> none  [stacked_from(): parts = lax.all_gather(parts, axes[k], axis=0, tiled=True)]
    all_to_all x1 -> x0, blocking collectives: 19.9 us -> none  [copy_for_each(): lax.all_to_all(jnp.broadcast_to(x[None], (peers, *x.shape)), axis, 0, 0,...]
    unnamed x10 -> x4, local copies, waits for them, and re-layouts: 11.2 us -> 0.01 us
    all_to_all x1 -> x0, starting transfers between devices: 9 us -> none  [copy_for_each(): lax.all_to_all(jnp.broadcast_to(x[None], (peers, *x.shape)), axis, 0, 0,...]
    all_to_all x1 -> x0, waiting for transfers between devices: 6.57 us -> none  [copy_for_each(): lax.all_to_all(jnp.broadcast_to(x[None], (peers, *x.shape)), axis, 0, 0,...]
  transfers between devices with their start and end apart: 7 -> 0, of which waited for: 6 -> 0; matrix products, arithmetic and copies ran while one was open for 2% -> 0% of each run, Pallas kernels for 0% -> 0%
where the time goes in v1:
time: 154 us; the launch traced here: 153 us
  Pallas kernels  136 us (88%)
  matrix products  14 us (9%)
  other arithmetic  2.1 us (1%)
    pallas_call x1, Pallas kernels, gather_projected(): pl.pallas_call(projected_kernel, name='gather_projected', out_shape=(jax....  62.7 us
    pallas_call x1, Pallas kernels, spread_direction(): pl.pallas_call(spread_kernel, name='spread_direction', out_shape=(jax.Sha...  51.5 us
    pallas_call x1, Pallas kernels, reduce_rows(): pl.pallas_call(reduce_kernel, name='reduce_rows', out_shape=jax.ShapeDtyp...  22.2 us
    dot_general x1, matrix products, per_device(): lifted = jnp.dot(ranks, full, preferred_element_type=jnp.float32)  9.65 us
    dot_general x1, matrix products, per_device(): lax.dot_general(projected, grads, (((0,), (0,)), ((), ())), preferred_ele...  4.38 us

profile of v1, /device:TPU:4, one launch (start us, length us, event | category | flops | bytes accessed | tf_op | source)
XLA Modules:
  0.0 153.2 jit_solution(1557417465335667720)
XLA Ops:
  0.6 62.7 %gather_projected.1 = (bf16[512,256]{1,0:T(8,128)(2,1)}, bf16[512,3328]{1,0:T(8,128)(2,1)}) custom-call(bf16[128,2048]{1,0:T(8,128)(2,1)} %inp.1, bf16[512,128]{1,0:T(8,128)(2,1)} %proj.3, bf16[128,3328]{1,0:T(8,128)(2,1)} %grads.1), custom_call_target="tpu_custom_call" | custom-call | tf_op jit(solution)/shard_map/gather_projected/pallas_call | solution.py:221
  63.3 0.0 copy-start
  63.3 0.0 copy-start.1
  63.3 4.4 %convolution_convert_fusion.part = bf16[256,3328]{1,0:T(8,128)(2,1)} fusion(bf16[512,256]{1,0:T(8,128)(2,1)} %get-tuple-element.7, bf16[512,3328]{1,0:T(8,128)(2,1)} %get-tuple-element.8), kind=kOutput, calls=%fused_computation.1 | convolution fusion | flops 873267200 | bytes 5373952 | tf_op jit(solution)/shard_map/dot_general | solution.py:471
  67.7 22.2 %reduce_rows.1 = f32[32,3328]{1,0:T(8,128)} custom-call(bf16[256,3328]{1,0:T(8,128)(2,1)} %convolution_convert_fusion.part), custom_call_target="tpu_custom_call" | custom-call | tf_op jit(solution)/shard_map/reduce_rows/pallas_call | solution.py:318
  89.9 0.0 copy-done
  89.9 0.0 copy-done.1
  89.9 2.1 %divide_convert_fusion = (bf16[32,3328]{1,0:T(8,128)(2,1)}, f32[32,3328]{1,0:T(8,128)}, f32[32,3328]{1,0:T(8,128)}) fusion(f32[32,3328]{1,0:T(8,128)} %reduce_rows.1, f32[32,3328]{1,0:T(8,128)S(1)} %copy-done, f32[32,3328]{1,0:T(8,128)S(1)} %copy-done.1), kind=kLoop, calls=%fused_computation.4 | loop fusion | flops 1171456 | bytes 2342912 | tf_op jit(solution)/shard_map/convert_element_type | solution.py:479
  92.0 51.5 %spread_direction.1 = (bf16[1024,3328]{1,0:T(8,128)(2,1)}, bf16[512,1024]{1,0:T(8,128)(2,1)}) custom-call(bf16[32,3328]{1,0:T(8,128)(2,1)} %get-tuple-element.11.own, bf16[512,128]{1,0:T(8,128)(2,1)} %proj.3), custom_call_target="tpu_custom_call" | custom-call | tf_op jit(solution)/shard_map/spread_direction/pallas_call | solution.py:448
  143.5 9.6 %subtract_convert_fusion = bf16[512,3328]{1,0:T(8,128)(2,1)} fusion(bf16[512,3328]{1,0:T(8,128)(2,1)} %param.9, bf16[512,1024]{1,0:T(8,128)(2,1)} %get-tuple-element.9, bf16[1024,3328]{1,0:T(8,128)(2,1)} %get-tuple-element.10), kind=kOutput, calls=%fused_computation | convolution fusion | flops 3496476672 | bytes 14680064 | tf_op jit(solution)/shard_map/dot_general | solution.py:483
Async XLA Ops:
  63.3 26.6 %copy-start = (f32[32,3328]{1,0:T(8,128)S(1)}, f32[32,3328]{1,0:T(8,128)}, u32[]{:S(2)}) copy-start(f32[32,3328]{1,0:T(8,128)} %param.11) | copy-start | bytes 1277956
  63.3 26.6 %copy-start.1 = (f32[32,3328]{1,0:T(8,128)S(1)}, f32[32,3328]{1,0:T(8,128)}, u32[]{:S(2)}) copy-start(f32[32,3328]{1,0:T(8,128)} %param.10) | copy-start | bytes 1277956

commit v2 on v1

v2 whole, which is shorter than its diff:
```python
import functools

import jax
import jax.numpy as jnp
from jax import lax
from jax.experimental import pallas as pl
from jax.experimental.pallas import tpu as pltpu
from jax.sharding import Mesh
from jax.sharding import PartitionSpec as P

STEP = 1000
AXES = ("dp_0", "dp_1", "dp_2", "mp_0", "mp_1")
DP = AXES[:3]
MP = AXES[3:]
MESH = pl.DeviceIdType.MESH
ANY = pl.BlockSpec(memory_space=pl.ANY)
VMEM = pl.BlockSpec(memory_space=pltpu.VMEM)
DMA = pltpu.SemaphoreType.DMA


def place():
    return tuple(lax.axis_index(a) for a in AXES)


def remote(src, dst, send_sem, recv_sem, **where):
    return pltpu.make_async_remote_copy(
        src_ref=src,
        dst_ref=dst,
        send_sem=send_sem,
        recv_sem=recv_sem,
        device_id=where,
        device_id_type=MESH,
    )


def landed(dst, sem):
    pltpu.make_async_copy(dst, dst, sem).wait()


def rows(start, size, unit=None):
    return pl.ds(pl.multiple_of(start, unit or size), size)


def greet(peers, extra=None):
    barrier = pltpu.get_barrier_semaphore()
    for peer in peers:
        pl.semaphore_signal(barrier, inc=1, device_id=peer, device_id_type=MESH)
    count = len(peers)
    if extra is not None:
        peer, present = extra

        @pl.when(present)
        def _():
            pl.semaphore_signal(barrier, inc=1, device_id=peer, device_id_type=MESH)

        count = count + present.astype(jnp.int32)
    pl.semaphore_wait(barrier, count)


def projected_kernel(
    inp, proj, grads, pa, g4,
    inp4, pt, pq, part, half_in, rs_in, g_own,
    loc_sem, inp_s, inp_r, g_s, g_r, pt_s, pt_r, pq_s, pq_r, half_s, half_r, rs_s, rs_r, pa_s, pa_r,
):
    y, x, zl, h, c = place()
    up, down = lax.rem(y + 1, 4), lax.rem(y + 3, 4)
    tok = inp.shape[0]
    half = tok // 2
    feat = proj.shape[0]
    lanes = proj.shape[1]
    peers = [{"dp_0": up}, {"dp_0": down}]
    for dx in range(4):
        for dz in range(2):
            for dc in range(2):
                if dx or dz or dc:
                    peers.append({
                        "dp_1": lax.rem(x + dx, 4),
                        "dp_2": lax.rem(zl + dz, 2),
                        "mp_1": lax.rem(c + dc, 2),
                    })
    for dh in range(1, 4):
        for dc in range(2):
            peers.append({"mp_0": lax.rem(h + dh, 4), "mp_1": lax.rem(c + dc, 2)})
    greet(peers, ({"dp_0": h, "mp_0": y}, y != h))

    in_up = remote(inp, inp4.at[1], inp_s.at[0], inp_r.at[0], dp_0=up)
    in_dn = remote(inp, inp4.at[3], inp_s.at[1], inp_r.at[1], dp_0=down)
    swap = remote(proj, pt, pt_s.at[0], pt_r.at[0], dp_0=h, mp_0=y)
    swap_here = pltpu.make_async_copy(proj, pt, pt_r.at[0])

    @pl.when(y != h)
    def _():
        swap.start()

    @pl.when(y == h)
    def _():
        swap_here.start()

    in_up.start()
    in_dn.start()
    own_in = pltpu.make_async_copy(inp, inp4.at[0], loc_sem.at[0])
    own_in.start()
    own_g = pltpu.make_async_copy(grads, g_own, loc_sem.at[1])
    own_g.start()

    landed(pt, pt_r.at[0])
    core = x // 2
    spot = pq.at[rows((lax.rem(x, 2) * 2 + zl) * feat, feat), rows(c * lanes, lanes)]
    mark = (lax.rem(x, 2) * 2 + zl) * 2 + c
    spread = []
    for dx in (1, 3, 2, 0):
        for dz in (1, 0):
            if dx or dz:
                cp = remote(
                    pt, spot, pq_s.at[dx * 2 + dz], pq_r.at[mark],
                    dp_1=lax.rem(x + dx, 4), dp_2=lax.rem(zl + dz, 2), mp_1=core,
                )
                cp.start()
                spread.append(cp)
    other = remote(pt, spot, pq_s.at[0], pq_r.at[mark], mp_1=1 - c)
    here = pltpu.make_async_copy(pt, spot, pq_r.at[mark])

    @pl.when(core != c)
    def _():
        other.start()

    @pl.when(core == c)
    def _():
        here.start()

    in_up.wait_recv()
    fw_up = remote(
        inp4.at[1, pl.ds(0, half)], inp4.at[2, pl.ds(0, half)], inp_s.at[2], inp_r.at[2], dp_0=up
    )
    fw_up.start()
    in_dn.wait_recv()
    fw_dn = remote(
        inp4.at[3, pl.ds(half, half)], inp4.at[2, pl.ds(half, half)], inp_s.at[3], inp_r.at[3], dp_0=down
    )
    fw_dn.start()
    g_up = remote(grads, g4.at[pl.ds(tok, tok)], g_s.at[0], g_r.at[0], dp_0=up)
    g_dn = remote(grads, g4.at[pl.ds(3 * tok, tok)], g_s.at[1], g_r.at[1], dp_0=down)
    g_up.start()
    g_dn.start()
    own_g.wait()
    put_g = pltpu.make_async_copy(g_own, g4.at[pl.ds(0, tok)], loc_sem.at[2])
    put_g.start()

    own_in.wait()
    for k in range(8):
        landed(pq.at[pl.ds((k // 2) * feat, feat), pl.ds((k % 2) * lanes, lanes)], pq_r.at[k])
    for b in (0, 1, 3):
        part[pl.ds(b * tok, tok)] = jnp.dot(inp4[b], pq[...], preferred_element_type=jnp.float32)
    fw_up.wait_recv()
    fw_dn.wait_recv()
    part[pl.ds(2 * tok, tok)] = jnp.dot(inp4[2], pq[...], preferred_element_type=jnp.float32)

    many = 2 * tok
    pair = remote(part.at[rows((1 - c) * many, many)], half_in, half_s.at[0], half_r.at[0], mp_1=1 - c)
    pair.start()
    pair.wait()
    mine = rows(c * many, many)
    part[mine] += half_in[...]
    cut = many // 4
    sums = []
    for dh in range(1, 4):
        to = lax.rem(h + dh, 4)
        cp = remote(
            part.at[rows(c * many + to * cut, cut)], rs_in.at[dh - 1], rs_s.at[dh - 1], rs_r.at[dh - 1], mp_0=to
        )
        cp.start()
        sums.append(cp)
    for cp in sums:
        cp.wait_recv()
    piece = rows(c * many + h * cut, cut)
    pa[piece] = (part[piece] + rs_in[0] + rs_in[1] + rs_in[2]).astype(pa.dtype)
    shares = []
    for dh in range(4):
        for dc in range(2):
            if dh or dc:
                k = dh * 2 + dc - 1
                cp = remote(
                    pa.at[piece], pa.at[piece], pa_s.at[k], pa_r.at[k],
                    mp_0=lax.rem(h + dh, 4), mp_1=lax.rem(c + dc, 2),
                )
                cp.start()
                shares.append(cp)

    g_up.wait_recv()
    gf_up = remote(
        g4.at[pl.ds(tok, half)], g4.at[pl.ds(2 * tok, half)], g_s.at[2], g_r.at[2], dp_0=up
    )
    gf_up.start()
    g_dn.wait_recv()
    gf_dn = remote(
        g4.at[pl.ds(3 * tok + half, half)], g4.at[pl.ds(2 * tok + half, half)], g_s.at[3], g_r.at[3], dp_0=down
    )
    gf_dn.start()

    for k in range(1, 8):
        frm_h, frm_c = lax.rem(h + 4 - k // 2, 4), lax.rem(c + 2 - k % 2, 2)
        landed(pa.at[rows(frm_c * many + frm_h * cut, cut)], pa_r.at[k - 1])
    gf_up.wait_recv()
    gf_dn.wait_recv()
    put_g.wait()
    for cp in (in_up, in_dn, fw_up, fw_dn, g_up, g_dn, gf_up, gf_dn, *spread, *sums, *shares):
        cp.wait_send()

    @pl.when(y != h)
    def _():
        swap.wait_send()

    @pl.when(core != c)
    def _():
        other.wait_send()


def gather_projected(inputs, projector, out_grads):
    tok, feats = inputs.shape
    feat, lanes = projector.shape
    cols = out_grads.shape[1]
    bf, f32 = jnp.bfloat16, jnp.float32
    return pl.pallas_call(
        projected_kernel,
        name="gather_projected",
        out_shape=(
            jax.ShapeDtypeStruct((4 * tok, 2 * lanes), bf),
            jax.ShapeDtypeStruct((4 * tok, cols), bf),
        ),
        in_specs=[ANY] * 3,
        out_specs=(VMEM, ANY),
        scratch_shapes=[
            pltpu.VMEM((4, tok, feats), bf),
            pltpu.VMEM((feat, lanes), bf),
            pltpu.VMEM((4 * feat, 2 * lanes), bf),
            pltpu.VMEM((4 * tok, 2 * lanes), f32),
            pltpu.VMEM((2 * tok, 2 * lanes), f32),
            pltpu.VMEM((3, tok // 2, 2 * lanes), f32),
            pltpu.VMEM((tok, cols), bf),
            DMA((3,)),
            DMA((4,)), DMA((4,)),
            DMA((4,)), DMA((4,)),
            DMA((1,)), DMA((1,)),
            DMA((8,)), DMA((8,)),
            DMA((1,)), DMA((1,)),
            DMA((3,)), DMA((3,)),
            DMA((7,)), DMA((7,)),
        ],
        compiler_params=pltpu.CompilerParams(collective_id=0, has_side_effects=True),
    )(inputs, projector, out_grads)


def update_kernel(
    chunks, part, first_m, second_m, proj, new_first, new_second, full, prow,
    raw_l, raw_r, via_l, via_r, turn_r, turn_l, add_l, add_r, zsend, zrecv, both, stage,
    loc_sem, put_sem, rs_s, rs_r, d_s, d_r, ag_s, ag_r, p_s, p_r,
):
    y, x, zl, h, c = place()
    n = first_m.shape[0]
    lanes = proj.shape[1]
    f32 = jnp.float32
    right, left, far = lax.rem(x + 1, 4), lax.rem(x + 3, 4), lax.rem(x + 2, 4)

    def plus(at, d):
        return lax.rem(at + d, 4)

    others = []
    for dh in range(4):
        for dc in range(2):
            if dh:
                others.append({"mp_0": plus(h, dh), "mp_1": lax.rem(c + dc, 2)})
            elif dc:
                others.append({"mp_1": 1 - c})
    peers = [{"dp_2": 1 - zl}]
    for axis, at in (("dp_0", y), ("dp_1", x)):
        peers += [{axis: plus(at, 1)}, {axis: plus(at, 3)}]
    greet(peers + others)

    sent = []
    flow = {}

    def send(name, src, dst, s, r, **where):
        cp = remote(src, dst, s, r, **where)
        cp.start()
        sent.append(cp)
        flow[name] = cp

    def cols(k):
        return pl.ds(chunks[k][0], chunks[k][1])

    def piece(k, of, half):
        return part.at[rows(of * 2 * n + half * n, n), cols(k)]

    def at(ref, k):
        return ref.at[:, cols(k)]

    def rs_far(k):
        send((k, 0), piece(k, far, 0), at(via_l, k), rs_s.at[k, 0], rs_r.at[k, 0], dp_1=right)
        send((k, 1), piece(k, far, 1), at(via_r, k), rs_s.at[k, 1], rs_r.at[k, 1], dp_1=left)

    def rs_near(k):
        send((k, 2), piece(k, right, 1), at(raw_l, k), rs_s.at[k, 2], rs_r.at[k, 2], dp_1=right)
        send((k, 3), piece(k, left, 0), at(raw_r, k), rs_s.at[k, 3], rs_r.at[k, 3], dp_1=left)

    def load(ref, k, where=slice(None)):
        return ref[where, cols(k)].astype(f32)

    def rs_turn(k):
        flow[k, 0].wait_recv()
        turn_r[:, cols(k)] = (load(via_l, k) + load(part, k, rows(right * 2 * n, n))).astype(turn_r.dtype)
        send((k, 4), at(turn_r, k), at(add_l, k), rs_s.at[k, 4], rs_r.at[k, 4], dp_1=right)
        flow[k, 1].wait_recv()
        turn_l[:, cols(k)] = (load(via_r, k) + load(part, k, rows(left * 2 * n + n, n, n))).astype(turn_l.dtype)
        send((k, 5), at(turn_l, k), at(add_r, k), rs_s.at[k, 5], rs_r.at[k, 5], dp_1=left)

    def total(k, half):
        if half == 0:
            return load(part, k, rows(x * 2 * n, n)) + load(add_l, k) + load(raw_r, k)
        return load(part, k, rows(x * 2 * n + n, n, n)) + load(add_r, k) + load(raw_l, k)

    def rs_sum(k):
        for i in (2, 3, 4, 5):
            flow[k, i].wait_recv()
        for mine in range(2):

            @pl.when(zl == mine)
            def _():
                zsend[:, cols(k)] = total(k, 1 - mine).astype(zsend.dtype)

        send((k, 6), at(zsend, k), at(zrecv, k), rs_s.at[k, 6], rs_r.at[k, 6], dp_2=1 - zl)
        for mine in range(2):

            @pl.when(zl == mine)
            def _():
                new_first[:, cols(k)] = total(k, mine)

    def adam(k):
        flow[k, 6].wait_recv()
        grad = new_first[:, cols(k)] + load(zrecv, k)
        m1 = 0.9 * first_m[:, cols(k)] + 0.1 * grad
        m2 = 0.999 * second_m[:, cols(k)] + 0.001 * grad * grad
        new_first[:, cols(k)] = m1
        new_second[:, cols(k)] = m2
        first_fix = 1.0 - 0.9**STEP
        second_fix = 1.0 - 0.999**STEP
        both[rows(zl * n, n), cols(k)] = (
            m1 / first_fix / (jnp.sqrt(m2 / second_fix) + 1e-08)
        ).astype(both.dtype)
        own = both.at[rows(zl * n, n), cols(k)]
        send((k, "d"), own, own, d_s.at[k], d_r.at[k], dp_2=1 - zl)

    def line(k):
        if chunks[k][2] == 0:
            return "dp_1", "dp_0", x, y, 1, 4
        return "dp_0", "dp_1", y, x, 4, 1

    def region(k, p1, p2, start, size):
        f1, f2 = line(k)[4:]
        return full.at[rows((p1 * f1 + p2 * f2) * 2 * n + start, size, n), cols(k)]

    def pass_on(k, i, axis, to, where, src=None):
        send((k, "a", i), where if src is None else src, where, ag_s.at[k, i], ag_r.at[k, i], **{axis: to})

    def ag_own(k):
        first, second, at1, at2 = line(k)[:4]
        landed(both.at[rows((1 - zl) * n, n), cols(k)], d_r.at[k])
        src, here = both.at[:, cols(k)], region(k, at1, at2, 0, 2 * n)
        pass_on(k, 0, first, plus(at1, 1), here, src)
        pass_on(k, 1, first, plus(at1, 3), here, src)
        pass_on(k, 4, second, plus(at2, 1), here, src)
        pass_on(k, 8, second, plus(at2, 3), here, src)
        pltpu.make_async_copy(src, here, put_sem.at[k]).start()

    def ag_first(k):
        first, second, at1, at2 = line(k)[:4]
        for j, d, to, half in ((0, 3, 1, 0), (1, 1, 3, 1)):
            landed(region(k, plus(at1, d), at2, 0, 2 * n), ag_r.at[k, j])
            pass_on(k, 2 + j, first, plus(at1, to), region(k, plus(at1, d), at2, half * n, n))
            here = region(k, plus(at1, d), at2, 0, 2 * n)
            pass_on(k, 5 + j, second, plus(at2, 1), here)
            pass_on(k, 9 + j, second, plus(at2, 3), here)

    def ag_far(k):
        first, second, at1, at2 = line(k)[:4]
        landed(region(k, plus(at1, 2), at2, 0, n), ag_r.at[k, 2])
        landed(region(k, plus(at1, 2), at2, n, n), ag_r.at[k, 3])
        here = region(k, plus(at1, 2), at2, 0, 2 * n)
        pass_on(k, 7, second, plus(at2, 1), here)
        pass_on(k, 11, second, plus(at2, 3), here)

    def ag_second(k, i):
        first, second, at1, at2 = line(k)[:4]
        d = (0, 3, 1, 2)[i]
        landed(region(k, plus(at1, d), plus(at2, 3), 0, 2 * n), ag_r.at[k, 4 + i])
        pass_on(k, 12 + i, second, plus(at2, 1), region(k, plus(at1, d), plus(at2, 3), 0, n))
        landed(region(k, plus(at1, d), plus(at2, 1), 0, 2 * n), ag_r.at[k, 8 + i])
        pass_on(k, 16 + i, second, plus(at2, 3), region(k, plus(at1, d), plus(at2, 1), n, n))

    def ag_last(k):
        first, second, at1, at2 = line(k)[:4]
        for i, d in enumerate((0, 3, 1, 2)):
            landed(region(k, plus(at1, d), plus(at2, 2), 0, n), ag_r.at[k, 12 + i])
            landed(region(k, plus(at1, d), plus(at2, 2), n, n), ag_r.at[k, 16 + i])
        landed(region(k, at1, at2, 0, 2 * n), put_sem.at[k])

    def own_rows():
        take.wait()
        keep.start()
        for i, who in enumerate(others):
            send(("p", i), stage, here, p_s.at[i], p_r.at[i], **who)

    take = pltpu.make_async_copy(proj, stage, loc_sem.at[0])
    take.start()
    here = prow.at[:, rows((h * 2 + c) * lanes, lanes)]
    keep = pltpu.make_async_copy(stage, here, loc_sem.at[1])

    rs_far(0)
    rs_near(0)
    rs_far(1)
    rs_turn(0)
    rs_near(1)
    rs_far(2)
    rs_sum(0)
    rs_turn(1)
    rs_near(2)
    adam(0)
    rs_sum(1)
    rs_turn(2)
    ag_own(0)
    adam(1)
    rs_sum(2)
    ag_own(1)
    adam(2)
    ag_first(0)
    ag_own(2)
    own_rows()
    ag_first(1)
    ag_far(0)
    ag_first(2)
    ag_far(1)
    ag_far(2)
    for i in range(4):
        for k in range(3):
            ag_second(k, i)
    for k in range(3):
        ag_last(k)
    for i, who in enumerate(others):
        frm = plus(h, 4 - (i + 1) // 2) * 2 + lax.rem(c + (i + 1) % 2, 2)
        landed(prow.at[:, rows(frm * lanes, lanes)], p_r.at[i])
    keep.wait()
    for cp in sent:
        cp.wait_send()


def update(part, first_moment, second_moment, projector):
    n, cols = first_moment.shape
    feat, lanes = projector.shape
    bf, f32 = jnp.bfloat16, jnp.float32
    third = cols // 384 * 128
    chunks = ((0, third, 0), (third, third, 0), (2 * third, cols - 2 * third, 1))
    slot = pltpu.VMEM((n, cols), bf)
    count = len(chunks)
    return pl.pallas_call(
        functools.partial(update_kernel, chunks),
        name="update",
        out_shape=(
            jax.ShapeDtypeStruct((n, cols), f32),
            jax.ShapeDtypeStruct((n, cols), f32),
            jax.ShapeDtypeStruct((32 * n, cols), bf),
            jax.ShapeDtypeStruct((feat, 8 * lanes), bf),
        ),
        in_specs=[VMEM, VMEM, VMEM, ANY],
        out_specs=(VMEM, VMEM, ANY, ANY),
        scratch_shapes=[slot] * 10 + [
            pltpu.VMEM((2 * n, cols), bf),
            pltpu.VMEM((feat, lanes), bf),
            DMA((2,)),
            DMA((count,)),
            DMA((count, 7)), DMA((count, 7)),
            DMA((count,)), DMA((count,)),
            DMA((count, 20)), DMA((count, 20)),
            DMA((7,)), DMA((7,)),
        ],
        compiler_params=pltpu.CompilerParams(
            collective_id=1, has_side_effects=True, vmem_limit_bytes=12 << 20
        ),
    )(part, first_moment, second_moment, projector)


def per_device(inputs, projector, out_grads, weights, first_moment, second_moment):
    projected, grads = gather_projected(inputs, projector, out_grads)
    part = lax.dot_general(
        projected, grads, (((0,), (0,)), ((), ())), preferred_element_type=jnp.float32
    ).astype(jnp.bfloat16)
    new_first, new_second, full, ranks = update(part, first_moment, second_moment, projector)
    lifted = jnp.dot(ranks, full, preferred_element_type=jnp.float32)
    new_weights = (weights.astype(jnp.float32) - 2.0 * lifted).astype(jnp.bfloat16)
    return (new_weights, new_first, new_second)


def solution(mesh):
    finer = Mesh(mesh.devices.reshape(4, 4, 2, 4, 2), AXES)
    spec = P(DP, MP)
    return jax.shard_map(
        per_device, mesh=finer, in_specs=(spec,) * 6, out_specs=(spec,) * 3, check_vma=False
    )
```

time: 154 us -> 138 us (0.90)
  Pallas kernels: 136 us -> 127 us
  matrix products: 14 us -> 8.43 us
  other arithmetic: 2.1 us -> 0 us
    pallas_call x2 -> x1, Pallas kernels: 73.7 us -> 64.2 us  [update(): pl.pallas_call(functools.partial(update_kernel, chunks), name='update', o...]
    dot_general x1, matrix products: 9.65 us -> 5.16 us  [per_device(): lifted = jnp.dot(ranks, full, preferred_element_type=jnp.float32)]
    convert_element_type x1 -> x0, other arithmetic: 2.1 us -> none  [per_device(): (new_first / first_fix / (jnp.sqrt(new_second / second_fix) + 1e-08)).ast...]
where the time goes in v2:
time: 138 us
  Pallas kernels  127 us (92%)
  matrix products  8.43 us (6%)
  local copies, waits for them, and re-layouts  1.53 us (1%)
    pallas_call x1, Pallas kernels, update(): pl.pallas_call(functools.partial(update_kernel, chunks), name='update', o...  64.2 us
    pallas_call x1, Pallas kernels, gather_projected(): pl.pallas_call(projected_kernel, name='gather_projected', out_shape=(jax....  62.7 us
    dot_general x1, matrix products, per_device(): lifted = jnp.dot(ranks, full, preferred_element_type=jnp.float32)  5.16 us
    dot_general x1, matrix products, per_device(): lax.dot_general(projected, grads, (((0,), (0,)), ((), ())), preferred_ele...  3.26 us

profile of v2, /device:TPU:4, one launch (start us, length us, event | category | flops | bytes accessed | tf_op | source)
XLA Modules:
  0.0 137.5 jit_solution(3524957344680543804)
XLA Ops:
  0.6 0.0 copy-start
  0.6 0.0 copy-start.2
  0.7 0.0 copy-start.1
  0.7 62.7 %gather_projected.1 = (bf16[512,256]{1,0:T(8,128)(2,1)}, bf16[512,3328]{1,0:T(8,128)(2,1)}) custom-call(bf16[128,2048]{1,0:T(8,128)(2,1)} %inp.1, bf16[512,128]{1,0:T(8,128)(2,1)} %proj.3, bf16[128,3328]{1,0:T(8,128)(2,1)} %grads.1), custom_call_target="tpu_custom_call" | custom-call | tf_op jit(solution)/shard_map/gather_projected/pallas_call | solution.py:223
  63.3 0.0 copy-start.3
  63.3 3.3 %convolution_convert_fusion.part = bf16[256,3328]{1,0:T(8,128)(2,1)S(1)} fusion(bf16[512,256]{1,0:T(8,128)(2,1)} %get-tuple-element.9, bf16[512,3328]{1,0:T(8,128)(2,1)} %get-tuple-element.10), kind=kOutput, calls=%fused_computation.1 | convolution fusion | flops 873267200 | bytes 5373952 | tf_op jit(solution)/shard_map/dot_general | solution.py:492
  66.6 0.0 copy-done
  66.6 0.0 copy-done.2
  66.6 0.0 copy-done.1
  66.6 64.2 %update.1 = (f32[32,3328]{1,0:T(8,128)S(1)}, f32[32,3328]{1,0:T(8,128)S(1)}, bf16[1024,3328]{1,0:T(8,128)(2,1)S(1)}, bf16[512,1024]{1,0:T(8,128)(2,1)S(1)}) custom-call(bf16[256,3328]{1,0:T(8,128)(2,1)S(1)} %convolution_convert_fusion.part, f32[32,3328]{1,0:T(8,128)S(1)} %copy-done.1, f32[32,3328]{1,0:T(8,128)S(1)} %copy-done.2, bf16[512,128]{1,0:T(8,128)(2,1)S(1)} %copy-done), custom_call_target="tpu_custom_call" | custom-call | tf_op jit(solution)/shard_map/update/pallas_call | solution.py:463
  130.9 0.0 copy-done.3
  130.9 5.2 %subtract_convert_fusion = bf16[512,3328]{1,0:T(8,128)(2,1)} fusion(bf16[512,3328]{1,0:T(8,128)(2,1)S(1)} %copy-done.3, bf16[512,1024]{1,0:T(8,128)(2,1)S(1)} %get-tuple-element.11, bf16[1024,3328]{1,0:T(8,128)(2,1)S(1)} %get-tuple-element.12), kind=kOutput, calls=%fused_computation | convolution fusion | flops 3496476672 | bytes 14680064 | tf_op jit(solution)/shard_map/dot_general | solution.py:496
  136.0 0.8 copy.11
  136.8 0.8 copy.12
Async XLA Ops:
  0.6 66.0 %copy-start = (bf16[512,128]{1,0:T(8,128)(2,1)S(1)}, bf16[512,128]{1,0:T(8,128)(2,1)}, u32[]{:S(2)}) copy-start(bf16[512,128]{1,0:T(8,128)(2,1)} %proj.3) | copy-start | bytes 393220
  0.6 66.0 %copy-start.2 = (f32[32,3328]{1,0:T(8,128)S(1)}, f32[32,3328]{1,0:T(8,128)}, u32[]{:S(2)}) copy-start(f32[32,3328]{1,0:T(8,128)} %second_m.1) | copy-start | bytes 1277956
  0.7 66.0 %copy-start.1 = (f32[32,3328]{1,0:T(8,128)S(1)}, f32[32,3328]{1,0:T(8,128)}, u32[]{:S(2)}) copy-start(f32[32,3328]{1,0:T(8,128)} %first_m.1) | copy-start | bytes 1277956
  63.3 67.5 %copy-start.3 = (bf16[512,3328]{1,0:T(8,128)(2,1)S(1)}, bf16[512,3328]{1,0:T(8,128)(2,1)}, u32[]{:S(2)}) copy-start(bf16[512,3328]{1,0:T(8,128)(2,1)} %param.9) | copy-start | bytes 10223620

commit v3 on v2

--- a/solution.py
+++ b/solution.py
@@ -16,6 +16,10 @@
 ANY = pl.BlockSpec(memory_space=pl.ANY)
 VMEM = pl.BlockSpec(memory_space=pltpu.VMEM)
 DMA = pltpu.SemaphoreType.DMA
+
+
+def in_hbm(x):
+    return pltpu.with_memory_space_constraint(x, pltpu.HBM)
 
 
 def place():
@@ -58,205 +62,274 @@
 
 
 def projected_kernel(
-    inp, proj, grads, pa, g4,
-    inp4, pt, pq, part, half_in, rs_in, g_own,
-    loc_sem, inp_s, inp_r, g_s, g_r, pt_s, pt_r, pq_s, pq_r, half_s, half_r, rs_s, rs_r, pa_s, pa_r,
+    inp, proj, grads, pa, ga,
+    inp4, pq, own, out_half, half_in, via_d, via_u, raw_d, raw_u, turn_u, turn_d, add_d, add_u, g_own,
+    loc_sem, in_s, in_r, g_s, g_r, sw_s, pq_r, ring_s, ring_r, half_s, half_r, rs_s, rs_r, sh_s, sh_r,
 ):
     y, x, zl, h, c = place()
     up, down = lax.rem(y + 1, 4), lax.rem(y + 3, 4)
+    right, left = lax.rem(x + 1, 4), lax.rem(x + 3, 4)
+    above, below = lax.rem(h + 1, 4), lax.rem(h + 3, 4)
     tok = inp.shape[0]
     half = tok // 2
-    feat = proj.shape[0]
-    lanes = proj.shape[1]
-    peers = [{"dp_0": up}, {"dp_0": down}]
-    for dx in range(4):
-        for dz in range(2):
-            for dc in range(2):
-                if dx or dz or dc:
-                    peers.append({
-                        "dp_1": lax.rem(x + dx, 4),
-                        "dp_2": lax.rem(zl + dz, 2),
-                        "mp_1": lax.rem(c + dc, 2),
-                    })
-    for dh in range(1, 4):
-        for dc in range(2):
-            peers.append({"mp_0": lax.rem(h + dh, 4), "mp_1": lax.rem(c + dc, 2)})
+    feat, lanes = proj.shape
+    wide = ga.shape[1]
+    peers = [
+        {"dp_0": up}, {"dp_0": down}, {"dp_1": right}, {"dp_1": left},
+        {"mp_0": above}, {"mp_0": below}, {"mp_1": 1 - c},
+        {"dp_2": 1 - zl},
+        {"dp_0": h, "mp_0": y, "mp_1": 1 - c},
+    ]
     greet(peers, ({"dp_0": h, "mp_0": y}, y != h))
 
-    in_up = remote(inp, inp4.at[1], inp_s.at[0], inp_r.at[0], dp_0=up)
-    in_dn = remote(inp, inp4.at[3], inp_s.at[1], inp_r.at[1], dp_0=down)
-    swap = remote(proj, pt, pt_s.at[0], pt_r.at[0], dp_0=h, mp_0=y)
-    swap_here = pltpu.make_async_copy(proj, pt, pt_r.at[0])
-
-    @pl.when(y != h)
+    sent = []
+
+    def send(src, dst, s, r, **where):
+        cp = remote(src, dst, s, r, **where)
+        cp.start()
+        sent.append(cp)
+        return cp
+
+    core = x // 2
+
+    def block(i, z, k):
+        return pq.at[rows((i * 2 + z) * feat, feat), pl.ds(k * lanes, lanes)]
+
+    def part_of(i, z, k, p):
+        return pq.at[rows((i * 2 + z) * feat + p * (feat // 2), feat // 2), pl.ds(k * lanes, lanes)]
+
+    spot = pq.at[rows((lax.rem(x, 2) * 2 + zl) * feat, feat), rows(c * lanes, lanes)]
+    mark = (lax.rem(x, 2) * 2 + zl) * 2 + c
+    at_home = (y == h) & (c == core)
+    swap = remote(proj, spot, sw_s.at[0], pq_r.at[mark], dp_0=h, mp_0=y, mp_1=core)
+    stay = pltpu.make_async_copy(proj, spot, pq_r.at[mark])
+
+    @pl.when(jnp.logical_not(at_home))
     def _():
         swap.start()
 
-    @pl.when(y == h)
+    @pl.when(at_home)
     def _():
-        swap_here.start()
-
-    in_up.start()
-    in_dn.start()
-    own_in = pltpu.make_async_copy(inp, inp4.at[0], loc_sem.at[0])
+        stay.start()
+
+    def slot(k, start, size):
+        return inp4.at[k // 2, pl.ds((k % 2) * tok + start, size)]
+
+    lo, hi = pl.ds(0, half), pl.ds(half, half)
+    in_up = send(inp.at[lo], slot(1, 0, half), in_s.at[0], in_r.at[0], dp_0=up)
+    in_dn = send(inp.at[hi], slot(3, half, half), in_s.at[1], in_r.at[1], dp_0=down)
+    in_up2 = send(inp.at[hi], slot(1, half, half), in_s.at[2], in_r.at[2], dp_0=up)
+    in_dn2 = send(inp.at[lo], slot(3, 0, half), in_s.at[3], in_r.at[3], dp_0=down)
+    own_in = pltpu.make_async_copy(inp, slot(0, 0, tok), loc_sem.at[0])
     own_in.start()
-    own_g = pltpu.make_async_copy(grads, g_own, loc_sem.at[1])
+    own_g = pltpu.make_async_copy(grads.at[:, pl.ds(0, wide)], g_own, loc_sem.at[1])
     own_g.start()
 
-    landed(pt, pt_r.at[0])
-    core = x // 2
-    spot = pq.at[rows((lax.rem(x, 2) * 2 + zl) * feat, feat), rows(c * lanes, lanes)]
-    mark = (lax.rem(x, 2) * 2 + zl) * 2 + c
-    spread = []
-    for dx in (1, 3, 2, 0):
-        for dz in (1, 0):
-            if dx or dz:
-                cp = remote(
-                    pt, spot, pq_s.at[dx * 2 + dz], pq_r.at[mark],
-                    dp_1=lax.rem(x + dx, 4), dp_2=lax.rem(zl + dz, 2), mp_1=core,
-                )
-                cp.start()
-                spread.append(cp)
-    other = remote(pt, spot, pq_s.at[0], pq_r.at[mark], mp_1=1 - c)
-    here = pltpu.make_async_copy(pt, spot, pq_r.at[mark])
-
-    @pl.when(core != c)
-    def _():
-        other.start()
-
-    @pl.when(core == c)
-    def _():
-        here.start()
-
+    def away(i):
+        return lax.rem(x + 4 - (2 * c + i), 4)
+
+    later = []
+
+    def ring(k, dz, stage):
+        z = lax.rem(zl + dz, 2)
+        for i in range(2):
+            m = (i * 2 + z) * 2 + k
+            whole = block(i, z, k)
+            if stage == 0:
+                fr = remote(whole, whole, ring_s.at[m, 0], pq_r.at[m], dp_1=right)
+                fl = remote(whole, whole, ring_s.at[m, 1], pq_r.at[m], dp_1=left)
+                both = (fr, fl)
+                if dz == 0:
+                    both = (remote(whole, whole, ring_s.at[m, 2], pq_r.at[m], dp_2=1 - zl), fr, fl)
+
+                @pl.when(away(i) == 0)
+                def _():
+                    landed(whole, pq_r.at[m])
+                    for cp in both:
+                        cp.start()
+
+                later.append((away(i) == 0, both))
+            if stage == 1:
+                for d, p, to in ((1, 0, right), (3, 1, left)):
+                    some = part_of(i, z, k, p)
+                    fw = remote(some, some, ring_s.at[m, p], ring_r.at[m, p], dp_1=to)
+
+                    @pl.when(away(i) == d)
+                    def _():
+                        landed(whole, pq_r.at[m])
+                        fw.start()
+
+                    later.append((away(i) == d, (fw,)))
+            if stage == 2:
+
+                @pl.when(away(i) == 2)
+                def _():
+                    landed(part_of(i, z, k, 0), ring_r.at[m, 0])
+                    landed(part_of(i, z, k, 1), ring_r.at[m, 1])
+
+    ring(0, 0, 0)
+    ring(1, 0, 0)
     in_up.wait_recv()
-    fw_up = remote(
-        inp4.at[1, pl.ds(0, half)], inp4.at[2, pl.ds(0, half)], inp_s.at[2], inp_r.at[2], dp_0=up
-    )
-    fw_up.start()
+    fw_up = send(slot(1, 0, half), slot(2, 0, half), in_s.at[4], in_r.at[4], dp_0=up)
     in_dn.wait_recv()
-    fw_dn = remote(
-        inp4.at[3, pl.ds(half, half)], inp4.at[2, pl.ds(half, half)], inp_s.at[3], inp_r.at[3], dp_0=down
-    )
-    fw_dn.start()
-    g_up = remote(grads, g4.at[pl.ds(tok, tok)], g_s.at[0], g_r.at[0], dp_0=up)
-    g_dn = remote(grads, g4.at[pl.ds(3 * tok, tok)], g_s.at[1], g_r.at[1], dp_0=down)
-    g_up.start()
-    g_dn.start()
+    fw_dn = send(slot(3, half, half), slot(2, half, half), in_s.at[5], in_r.at[5], dp_0=down)
+    ring(0, 1, 0)
+    ring(1, 1, 0)
+
+    def g_from(start, size):
+        return ga.at[pl.ds(start, size)]
+
+    g_up = send(grads.at[lo, pl.ds(0, wide)], g_from(tok, half), g_s.at[0], g_r.at[0], dp_0=up)
+    g_dn = send(grads.at[hi, pl.ds(0, wide)], g_from(3 * tok + half, half), g_s.at[1], g_r.at[1], dp_0=down)
+    g_up2 = send(grads.at[hi, pl.ds(0, wide)], g_from(tok + half, half), g_s.at[2], g_r.at[2], dp_0=up)
+    g_dn2 = send(grads.at[lo, pl.ds(0, wide)], g_from(3 * tok, half), g_s.at[3], g_r.at[3], dp_0=down)
     own_g.wait()
-    put_g = pltpu.make_async_copy(g_own, g4.at[pl.ds(0, tok)], loc_sem.at[2])
+    put_g = pltpu.make_async_copy(g_own, g_from(0, tok), loc_sem.at[2])
     put_g.start()
-
+    for k in range(2):
+        for dz in range(2):
+            ring(k, dz, 1)
     own_in.wait()
-    for k in range(8):
-        landed(pq.at[pl.ds((k // 2) * feat, feat), pl.ds((k % 2) * lanes, lanes)], pq_r.at[k])
-    for b in (0, 1, 3):
-        part[pl.ds(b * tok, tok)] = jnp.dot(inp4[b], pq[...], preferred_element_type=jnp.float32)
+    in_up2.wait_recv()
+    in_dn2.wait_recv()
     fw_up.wait_recv()
     fw_dn.wait_recv()
-    part[pl.ds(2 * tok, tok)] = jnp.dot(inp4[2], pq[...], preferred_element_type=jnp.float32)
-
-    many = 2 * tok
-    pair = remote(part.at[rows((1 - c) * many, many)], half_in, half_s.at[0], half_r.at[0], mp_1=1 - c)
-    pair.start()
-    pair.wait()
-    mine = rows(c * many, many)
-    part[mine] += half_in[...]
-    cut = many // 4
-    sums = []
-    for dh in range(1, 4):
-        to = lax.rem(h + dh, 4)
-        cp = remote(
-            part.at[rows(c * many + to * cut, cut)], rs_in.at[dh - 1], rs_s.at[dh - 1], rs_r.at[dh - 1], mp_0=to
-        )
-        cp.start()
-        sums.append(cp)
-    for cp in sums:
-        cp.wait_recv()
-    piece = rows(c * many + h * cut, cut)
-    pa[piece] = (part[piece] + rs_in[0] + rs_in[1] + rs_in[2]).astype(pa.dtype)
-    shares = []
-    for dh in range(4):
-        for dc in range(2):
-            if dh or dc:
-                k = dh * 2 + dc - 1
-                cp = remote(
-                    pa.at[piece], pa.at[piece], pa_s.at[k], pa_r.at[k],
-                    mp_0=lax.rem(h + dh, 4), mp_1=lax.rem(c + dc, 2),
-                )
-                cp.start()
-                shares.append(cp)
-
+
+    pairs = []
+    for k in range(2):
+        for dz in range(2):
+            ring(k, dz, 2)
+        here = pl.ds(k * lanes, lanes)
+        for t in range(2):
+            out_half[k, pl.ds(t * tok, tok)] = jnp.dot(
+                inp4[1 - c, pl.ds(t * tok, tok)], pq[:, here], preferred_element_type=jnp.float32
+            )
+        pairs.append(send(out_half.at[k], half_in.at[k], half_s.at[k], half_r.at[k], mp_1=1 - c))
+        for t in range(2):
+            own[k, pl.ds(t * tok, tok)] = jnp.dot(
+                inp4[c, pl.ds(t * tok, tok)], pq[:, here], preferred_element_type=jnp.float32
+            )
+
+    cut = 2 * tok // 4
+    q = cut // 2
+    beyond = lax.rem(h + 2, 4)
+    flow = {}
+
+    def piece(k, of, p):
+        return own.at[k, rows(of * cut + p * q, q)]
+
+    def value(k, of, p):
+        return own[k, rows(of * cut + p * q, q)]
+
+    for k in range(2):
+        pairs[k].wait_recv()
+        own[k] += half_in[k]
+        flow[k, 0] = send(piece(k, beyond, 0), via_d.at[k], rs_s.at[k, 0], rs_r.at[k, 0], mp_0=above)
+        flow[k, 1] = send(piece(k, beyond, 1), via_u.at[k], rs_s.at[k, 1], rs_r.at[k, 1], mp_0=below)
+        flow[k, 2] = send(piece(k, above, 1), raw_d.at[k], rs_s.at[k, 2], rs_r.at[k, 2], mp_0=above)
+        flow[k, 3] = send(piece(k, below, 0), raw_u.at[k], rs_s.at[k, 3], rs_r.at[k, 3], mp_0=below)
+    for k in range(2):
+        flow[k, 0].wait_recv()
+        turn_u[k] = via_d[k] + value(k, above, 0)
+        flow[k, 4] = send(turn_u.at[k], add_d.at[k], rs_s.at[k, 4], rs_r.at[k, 4], mp_0=above)
+        flow[k, 1].wait_recv()
+        turn_d[k] = via_u[k] + value(k, below, 1)
+        flow[k, 5] = send(turn_d.at[k], add_u.at[k], rs_s.at[k, 5], rs_r.at[k, 5], mp_0=below)
+
+    def share(k, of, start=0, size=cut, who=c):
+        return pa.at[rows(who * 2 * tok + of * cut + start, size, size), pl.ds(k * lanes, lanes)]
+
+    for k in range(2):
+        for i in (2, 3, 4, 5):
+            flow[k, i].wait_recv()
+        top = value(k, h, 0) + add_d[k] + raw_u[k]
+        low = value(k, h, 1) + add_u[k] + raw_d[k]
+        pa[rows(c * 2 * tok + h * cut, cut), pl.ds(k * lanes, lanes)] = jnp.concatenate(
+            [top, low], axis=0
+        ).astype(pa.dtype)
+        flow[k, 6] = send(share(k, h), share(k, h), sh_s.at[k, 0], sh_r.at[k, 0], mp_0=above)
+        flow[k, 7] = send(share(k, h), share(k, h), sh_s.at[k, 1], sh_r.at[k, 1], mp_0=below)
+        send(share(k, h), share(k, h), sh_s.at[k, 4], sh_r.at[k, 4], mp_1=1 - c)
     g_up.wait_recv()
-    gf_up = remote(
-        g4.at[pl.ds(tok, half)], g4.at[pl.ds(2 * tok, half)], g_s.at[2], g_r.at[2], dp_0=up
+    gf_up = send(g_from(tok, half), g_from(2 * tok, half), g_s.at[4], g_r.at[4], dp_0=up)
+    g_dn.wait_recv()
+    gf_dn = send(
+        g_from(3 * tok + half, half), g_from(2 * tok + half, half), g_s.at[5], g_r.at[5], dp_0=down
     )
-    gf_up.start()
-    g_dn.wait_recv()
-    gf_dn = remote(
-        g4.at[pl.ds(3 * tok + half, half)], g4.at[pl.ds(2 * tok + half, half)], g_s.at[3], g_r.at[3], dp_0=down
-    )
-    gf_dn.start()
-
-    for k in range(1, 8):
-        frm_h, frm_c = lax.rem(h + 4 - k // 2, 4), lax.rem(c + 2 - k % 2, 2)
-        landed(pa.at[rows(frm_c * many + frm_h * cut, cut)], pa_r.at[k - 1])
+    for k in range(2):
+        landed(share(k, below), sh_r.at[k, 0])
+        send(share(k, below, 0, q), share(k, below, 0, q), sh_s.at[k, 2], sh_r.at[k, 2], mp_0=above)
+        send(share(k, below), share(k, below), sh_s.at[k, 5], sh_r.at[k, 5], mp_1=1 - c)
+        landed(share(k, above), sh_r.at[k, 1])
+        send(share(k, above, q, q), share(k, above, q, q), sh_s.at[k, 3], sh_r.at[k, 3], mp_0=below)
+        send(share(k, above), share(k, above), sh_s.at[k, 6], sh_r.at[k, 6], mp_1=1 - c)
+    for k in range(2):
+        landed(share(k, beyond, 0, q), sh_r.at[k, 2])
+        landed(share(k, beyond, q, q), sh_r.at[k, 3])
+        send(share(k, beyond), share(k, beyond), sh_s.at[k, 7], sh_r.at[k, 7], mp_1=1 - c)
+    for k in range(2):
+        for i, of in enumerate((h, below, above, beyond)):
+            landed(share(k, of, who=1 - c), sh_r.at[k, 4 + i])
+    g_up2.wait_recv()
+    g_dn2.wait_recv()
     gf_up.wait_recv()
     gf_dn.wait_recv()
     put_g.wait()
-    for cp in (in_up, in_dn, fw_up, fw_dn, g_up, g_dn, gf_up, gf_dn, *spread, *sums, *shares):
+    for cp in sent:
         cp.wait_send()
-
-    @pl.when(y != h)
-    def _():
-        swap.wait_send()
-
-    @pl.when(core != c)
-    def _():
-        other.wait_send()
+    for when, copies in later + [(jnp.logical_not(at_home), (swap,))]:
+
+        @pl.when(when)
+        def _():
+            for cp in copies:
+                cp.wait_send()
 
 
 def gather_projected(inputs, projector, out_grads):
     tok, feats = inputs.shape
     feat, lanes = projector.shape
-    cols = out_grads.shape[1]
+    wide = out_grads.shape[1]
     bf, f32 = jnp.bfloat16, jnp.float32
+    small = pltpu.VMEM((2, tok // 4, lanes), f32)
     return pl.pallas_call(
         projected_kernel,
         name="gather_projected",
         out_shape=(
             jax.ShapeDtypeStruct((4 * tok, 2 * lanes), bf),
-            jax.ShapeDtypeStruct((4 * tok, cols), bf),
+            jax.ShapeDtypeStruct((4 * tok, wide), bf),
         ),
         in_specs=[ANY] * 3,
         out_specs=(VMEM, ANY),
         scratch_shapes=[
-            pltpu.VMEM((4, tok, feats), bf),
-            pltpu.VMEM((feat, lanes), bf),
+            pltpu.VMEM((2, 2 * tok, feats), bf),
             pltpu.VMEM((4 * feat, 2 * lanes), bf),
-            pltpu.VMEM((4 * tok, 2 * lanes), f32),
-            pltpu.VMEM((2 * tok, 2 * lanes), f32),
-            pltpu.VMEM((3, tok // 2, 2 * lanes), f32),
-            pltpu.VMEM((tok, cols), bf),
+            pltpu.VMEM((2, 2 * tok, lanes), f32),
+            pltpu.VMEM((2, 2 * tok, lanes), f32),
+            pltpu.VMEM((2, 2 * tok, lanes), f32),
+            *[small] * 8,
+            pltpu.VMEM((tok, wide), bf),
             DMA((3,)),
-            DMA((4,)), DMA((4,)),
-            DMA((4,)), DMA((4,)),
-            DMA((1,)), DMA((1,)),
-            DMA((8,)), DMA((8,)),
-            DMA((1,)), DMA((1,)),
-            DMA((3,)), DMA((3,)),
-            DMA((7,)), DMA((7,)),
+            DMA((6,)), DMA((6,)),
+            DMA((6,)), DMA((6,)),
+            DMA((1,)), DMA((8,)),
+            DMA((8, 3)), DMA((8, 2)),
+            DMA((2,)), DMA((2,)),
+            DMA((2, 6)), DMA((2, 6)),
+            DMA((2, 8)), DMA((2, 8)),
         ],
-        compiler_params=pltpu.CompilerParams(collective_id=0, has_side_effects=True),
-    )(inputs, projector, out_grads)
+        compiler_params=pltpu.CompilerParams(
+            collective_id=0, has_side_effects=True, vmem_limit_bytes=12 << 20
+        ),
+    )(in_hbm(inputs), in_hbm(projector), in_hbm(out_grads))
 
 
 def update_kernel(
-    chunks, part, first_m, second_m, proj, new_first, new_second, full, prow,
-    raw_l, raw_r, via_l, via_r, turn_r, turn_l, add_l, add_r, zsend, zrecv, both, stage,
+    chunks, part, first_in, second_in, proj, new_first, new_second, full, prow,
+    raw_l, raw_r, via_l, via_r, turn_r, turn_l, add_l, add_r, zsend, zrecv, both, stage, first_m, second_m,
     loc_sem, put_sem, rs_s, rs_r, d_s, d_r, ag_s, ag_r, p_s, p_r,
 ):
     y, x, zl, h, c = place()
-    n = first_m.shape[0]
+    n = first_in.shape[0]
     lanes = proj.shape[1]
     f32 = jnp.float32
     right, left, far = lax.rem(x + 1, 4), lax.rem(x + 3, 4), lax.rem(x + 2, 4)
@@ -291,6 +364,9 @@
     def piece(k, of, half):
         return part.at[rows(of * 2 * n + half * n, n), cols(k)]
 
+    def mine_of(k, start):
+        return part[rows(start, n), cols(k)].astype(f32)
+
     def at(ref, k):
         return ref.at[:, cols(k)]
 
@@ -307,16 +383,16 @@
 
     def rs_turn(k):
         flow[k, 0].wait_recv()
-        turn_r[:, cols(k)] = (load(via_l, k) + load(part, k, rows(right * 2 * n, n))).astype(turn_r.dtype)
+        turn_r[:, cols(k)] = (load(via_l, k) + mine_of(k, right * 2 * n)).astype(turn_r.dtype)
         send((k, 4), at(turn_r, k), at(add_l, k), rs_s.at[k, 4], rs_r.at[k, 4], dp_1=right)
         flow[k, 1].wait_recv()
-        turn_l[:, cols(k)] = (load(via_r, k) + load(part, k, rows(left * 2 * n + n, n, n))).astype(turn_l.dtype)
+        turn_l[:, cols(k)] = (load(via_r, k) + mine_of(k, left * 2 * n + n)).astype(turn_l.dtype)
         send((k, 5), at(turn_l, k), at(add_r, k), rs_s.at[k, 5], rs_r.at[k, 5], dp_1=left)
 
     def total(k, half):
         if half == 0:
-            return load(part, k, rows(x * 2 * n, n)) + load(add_l, k) + load(raw_r, k)
-        return load(part, k, rows(x * 2 * n + n, n, n)) + load(add_r, k) + load(raw_l, k)
+            return mine_of(k, x * 2 * n) + load(add_l, k) + load(raw_r, k)
+        return mine_of(k, x * 2 * n + n) + load(add_r, k) + load(raw_l, k)
 
     def rs_sum(k):
         for i in (2, 3, 4, 5):
@@ -409,6 +485,12 @@
         for i, who in enumerate(others):
             send(("p", i), stage, here, p_s.at[i], p_r.at[i], **who)
 
+    state = [
+        pltpu.make_async_copy(first_in, first_m, loc_sem.at[2]),
+        pltpu.make_async_copy(second_in, second_m, loc_sem.at[3]),
+    ]
+    for cp in state:
+        cp.start()
     take = pltpu.make_async_copy(proj, stage, loc_sem.at[0])
     take.start()
     here = prow.at[:, rows((h * 2 + c) * lanes, lanes)]
@@ -423,6 +505,8 @@
     rs_sum(0)
     rs_turn(1)
     rs_near(2)
+    for cp in state:
+        cp.wait()
     adam(0)
     rs_sum(1)
     rs_turn(2)
@@ -452,12 +536,16 @@
         cp.wait_send()
 
 
+def split(cols):
+    third = cols // 384 * 128
+    return ((0, third, 0), (third, third, 0), (2 * third, cols - 2 * third, 1))
+
+
 def update(part, first_moment, second_moment, projector):
     n, cols = first_moment.shape
     feat, lanes = projector.shape
     bf, f32 = jnp.bfloat16, jnp.float32
-    third = cols // 384 * 128
-    chunks = ((0, third, 0), (third, third, 0), (2 * third, cols - 2 * third, 1))
+    chunks = split(cols)
     slot = pltpu.VMEM((n, cols), bf)
     count = len(chunks)
     return pl.pallas_call(
@@ -469,12 +557,14 @@
             jax.ShapeDtypeStruct((32 * n, cols), bf),
             jax.ShapeDtypeStruct((feat, 8 * lanes), bf),
         ),
-        in_specs=[VMEM, VMEM, VMEM, ANY],
+        in_specs=[VMEM, ANY, ANY, ANY],
         out_specs=(VMEM, VMEM, ANY, ANY),
         scratch_shapes=[slot] * 10 + [
             pltpu.VMEM((2 * n, cols), bf),
             pltpu.VMEM((feat, lanes), bf),
-            DMA((2,)),
+            pltpu.VMEM((n, cols), f32),
+            pltpu.VMEM((n, cols), f32),
+            DMA((4,)),
             DMA((count,)),
             DMA((count, 7)), DMA((count, 7)),
             DMA((count,)), DMA((count,)),
@@ -482,9 +572,9 @@
             DMA((7,)), DMA((7,)),
         ],
         compiler_params=pltpu.CompilerParams(
-            collective_id=1, has_side_effects=True, vmem_limit_bytes=12 << 20
+            collective_id=1, has_side_effects=True, vmem_limit_bytes=16 << 20
         ),
-    )(part, first_moment, second_moment, projector)
+    )(part, *(in_hbm(v) for v in (first_moment, second_moment, projector)))
 
 
 def per_device(inputs, projector, out_grads, weights, first_moment, second_moment):

time: 138 us -> 130 us (0.942)
  Pallas kernels: 127 us -> 121 us
  matrix products: 8.43 us -> 6.25 us
    pallas_call x1, Pallas kernels: 62.7 us -> 57.8 us  [gather_projected(): pl.pallas_call(projected_kernel, name='gather_projected', out_shape=(jax....]
    dot_general x1, matrix products: 3.26 us -> 1.09 us  [per_device(): lax.dot_general(projected, grads, (((0,), (0,)), ((), ())), preferred_ele...]
where the time goes in v3:
time: 130 us
  Pallas kernels  121 us (93%)
  matrix products  6.25 us (5%)
  local copies, waits for them, and re-layouts  1.52 us (1%)
    pallas_call x1, Pallas kernels, update(): pl.pallas_call(functools.partial(update_kernel, chunks), name='update', o...  63.6 us
    pallas_call x1, Pallas kernels, gather_projected(): pl.pallas_call(projected_kernel, name='gather_projected', out_shape=(jax....  57.8 us
    dot_general x1, matrix products, per_device(): lifted = jnp.dot(ranks, full, preferred_element_type=jnp.float32)  5.16 us

profile of v3, /device:TPU:4, one launch (start us, length us, event | category | flops | bytes accessed | tf_op | source)
XLA Modules:
  0.0 129.8 jit_solution(9153519629977785772)
XLA Ops:
  0.6 57.8 %gather_projected.1 = (bf16[512,256]{1,0:T(8,128)(2,1)S(1)}, bf16[512,3328]{1,0:T(8,128)(2,1)S(1)}) custom-call(bf16[128,2048]{1,0:T(8,128)(2,1)} %inp.1, bf16[512,128]{1,0:T(8,128)(2,1)} %proj.3, bf16[128,3328]{1,0:T(8,128)(2,1)} %grads.1), custom_call_target="tpu_custom_call" | custom-call | tf_op jit(solution)/shard_map/gather_projected/pallas_call | solution.py:294
  58.4 0.0 copy-start
  58.4 1.1 convolution_convert_fusion.part
  59.5 63.6 %update.1 = (f32[32,3328]{1,0:T(8,128)S(1)}, f32[32,3328]{1,0:T(8,128)S(1)}, bf16[1024,3328]{1,0:T(8,128)(2,1)S(1)}, bf16[512,1024]{1,0:T(8,128)(2,1)S(1)}) custom-call(bf16[256,3328]{1,0:T(8,128)(2,1)S(1)} %convolution_convert_fusion.part, f32[32,3328]{1,0:T(8,128)} %first_in.1, f32[32,3328]{1,0:T(8,128)} %second_in.1, bf16[512,128]{1,0:T(8,128)(2,1)} %proj.3), custom_call_target="tpu_custom_call" | custom-call | tf_op jit(solution)/shard_map/update/pallas_call | solution.py:551
  123.1 0.0 copy-done
  123.1 5.2 %subtract_convert_fusion = bf16[512,3328]{1,0:T(8,128)(2,1)} fusion(bf16[512,3328]{1,0:T(8,128)(2,1)S(1)} %copy-done, bf16[512,1024]{1,0:T(8,128)(2,1)S(1)} %get-tuple-element.11, bf16[1024,3328]{1,0:T(8,128)(2,1)S(1)} %get-tuple-element.12), kind=kOutput, calls=%fused_computation | convolution fusion | flops 3496476672 | bytes 14680064 | tf_op jit(solution)/shard_map/dot_general | solution.py:586
  128.3 0.8 copy.11
  129.1 0.8 copy.12
Async XLA Ops:
  58.4 64.7 %copy-start = (bf16[512,3328]{1,0:T(8,128)(2,1)S(1)}, bf16[512,3328]{1,0:T(8,128)(2,1)}, u32[]{:S(2)}) copy-start(bf16[512,3328]{1,0:T(8,128)(2,1)} %param.9) | copy-start | bytes 10223620

commit v4 on v3

--- a/solution.py
+++ b/solution.py
@@ -61,9 +61,9 @@
     pl.semaphore_wait(barrier, count)
 
 
-def projected_kernel(
+def projected_body(
     inp, proj, grads, pa, ga,
-    inp4, pq, own, out_half, half_in, via_d, via_u, raw_d, raw_u, turn_u, turn_d, add_d, add_u, g_own,
+    inp4, pq, own, out_half, half_in, via_d, via_u, raw_d, raw_u, turn_u, turn_d, add_d, add_u,
     loc_sem, in_s, in_r, g_s, g_r, sw_s, pq_r, ring_s, ring_r, half_s, half_r, rs_s, rs_r, sh_s, sh_r,
 ):
     y, x, zl, h, c = place()
@@ -74,14 +74,6 @@
     half = tok // 2
     feat, lanes = proj.shape
     wide = ga.shape[1]
-    peers = [
-        {"dp_0": up}, {"dp_0": down}, {"dp_1": right}, {"dp_1": left},
-        {"mp_0": above}, {"mp_0": below}, {"mp_1": 1 - c},
-        {"dp_2": 1 - zl},
-        {"dp_0": h, "mp_0": y, "mp_1": 1 - c},
-    ]
-    greet(peers, ({"dp_0": h, "mp_0": y}, y != h))
-
     sent = []
 
     def send(src, dst, s, r, **where):
@@ -122,7 +114,7 @@
     in_dn2 = send(inp.at[lo], slot(3, 0, half), in_s.at[3], in_r.at[3], dp_0=down)
     own_in = pltpu.make_async_copy(inp, slot(0, 0, tok), loc_sem.at[0])
     own_in.start()
-    own_g = pltpu.make_async_copy(grads.at[:, pl.ds(0, wide)], g_own, loc_sem.at[1])
+    own_g = pltpu.make_async_copy(grads, ga.at[pl.ds(0, tok)], loc_sem.at[1])
     own_g.start()
 
     def away(i):
@@ -183,9 +175,6 @@
     g_dn = send(grads.at[hi, pl.ds(0, wide)], g_from(3 * tok + half, half), g_s.at[1], g_r.at[1], dp_0=down)
     g_up2 = send(grads.at[hi, pl.ds(0, wide)], g_from(tok + half, half), g_s.at[2], g_r.at[2], dp_0=up)
     g_dn2 = send(grads.at[lo, pl.ds(0, wide)], g_from(3 * tok, half), g_s.at[3], g_r.at[3], dp_0=down)
-    own_g.wait()
-    put_g = pltpu.make_async_copy(g_own, g_from(0, tok), loc_sem.at[2])
-    put_g.start()
     for k in range(2):
         for dz in range(2):
             ring(k, dz, 1)
@@ -199,16 +188,12 @@
     for k in range(2):
         for dz in range(2):
             ring(k, dz, 2)
-        here = pl.ds(k * lanes, lanes)
-        for t in range(2):
-            out_half[k, pl.ds(t * tok, tok)] = jnp.dot(
-                inp4[1 - c, pl.ds(t * tok, tok)], pq[:, here], preferred_element_type=jnp.float32
-            )
+        out_half[k] = jnp.dot(
+            inp4[1 - c], pq[:, pl.ds(k * lanes, lanes)], preferred_element_type=jnp.float32
+        )
         pairs.append(send(out_half.at[k], half_in.at[k], half_s.at[k], half_r.at[k], mp_1=1 - c))
-        for t in range(2):
-            own[k, pl.ds(t * tok, tok)] = jnp.dot(
-                inp4[c, pl.ds(t * tok, tok)], pq[:, here], preferred_element_type=jnp.float32
-            )
+    for k in range(2):
+        own[k] = jnp.dot(inp4[c], pq[:, pl.ds(k * lanes, lanes)], preferred_element_type=jnp.float32)
 
     cut = 2 * tok // 4
     q = cut // 2
@@ -274,80 +259,34 @@
     g_dn2.wait_recv()
     gf_up.wait_recv()
     gf_dn.wait_recv()
-    put_g.wait()
-    for cp in sent:
-        cp.wait_send()
-    for when, copies in later + [(jnp.logical_not(at_home), (swap,))]:
-
-        @pl.when(when)
-        def _():
-            for cp in copies:
-                cp.wait_send()
-
-
-def gather_projected(inputs, projector, out_grads):
-    tok, feats = inputs.shape
-    feat, lanes = projector.shape
-    wide = out_grads.shape[1]
-    bf, f32 = jnp.bfloat16, jnp.float32
-    small = pltpu.VMEM((2, tok // 4, lanes), f32)
-    return pl.pallas_call(
-        projected_kernel,
-        name="gather_projected",
-        out_shape=(
-            jax.ShapeDtypeStruct((4 * tok, 2 * lanes), bf),
-            jax.ShapeDtypeStruct((4 * tok, wide), bf),
-        ),
-        in_specs=[ANY] * 3,
-        out_specs=(VMEM, ANY),
-        scratch_shapes=[
-            pltpu.VMEM((2, 2 * tok, feats), bf),
-            pltpu.VMEM((4 * feat, 2 * lanes), bf),
-            pltpu.VMEM((2, 2 * tok, lanes), f32),
-            pltpu.VMEM((2, 2 * tok, lanes), f32),
-            pltpu.VMEM((2, 2 * tok, lanes), f32),
-            *[small] * 8,
-            pltpu.VMEM((tok, wide), bf),
-            DMA((3,)),
-            DMA((6,)), DMA((6,)),
-            DMA((6,)), DMA((6,)),
-            DMA((1,)), DMA((8,)),
-            DMA((8, 3)), DMA((8, 2)),
-            DMA((2,)), DMA((2,)),
-            DMA((2, 6)), DMA((2, 6)),
-            DMA((2, 8)), DMA((2, 8)),
-        ],
-        compiler_params=pltpu.CompilerParams(
-            collective_id=0, has_side_effects=True, vmem_limit_bytes=12 << 20
-        ),
-    )(in_hbm(inputs), in_hbm(projector), in_hbm(out_grads))
-
-
-def update_kernel(
-    chunks, part, first_in, second_in, proj, new_first, new_second, full, prow,
-    raw_l, raw_r, via_l, via_r, turn_r, turn_l, add_l, add_r, zsend, zrecv, both, stage, first_m, second_m,
-    loc_sem, put_sem, rs_s, rs_r, d_s, d_r, ag_s, ag_r, p_s, p_r,
+    own_g.wait()
+
+    def finish():
+        for cp in sent:
+            cp.wait_send()
+        for when, copies in later + [(jnp.logical_not(at_home), (swap,))]:
+
+            @pl.when(when)
+            def _():
+                for cp in copies:
+                    cp.wait_send()
+
+    return finish
+
+
+def update_body(
+    chunks, early, pa, ga, proj, new_first, new_second, full, prow,
+    part, raw_l, raw_r, via_l, via_r, turn_r, turn_l, add_l, add_r, zsend, zrecv, both, stage, first_m, second_m,
+    keep_sem, put_sem, rs_s, rs_r, d_s, d_r, ag_s, ag_r, p_s, p_r,
 ):
     y, x, zl, h, c = place()
-    n = first_in.shape[0]
+    n = first_m.shape[0]
     lanes = proj.shape[1]
     f32 = jnp.float32
     right, left, far = lax.rem(x + 1, 4), lax.rem(x + 3, 4), lax.rem(x + 2, 4)
 
     def plus(at, d):
         return lax.rem(at + d, 4)
-
-    others = []
-    for dh in range(4):
-        for dc in range(2):
-            if dh:
-                others.append({"mp_0": plus(h, dh), "mp_1": lax.rem(c + dc, 2)})
-            elif dc:
-                others.append({"mp_1": 1 - c})
-    peers = [{"dp_2": 1 - zl}]
-    for axis, at in (("dp_0", y), ("dp_1", x)):
-        peers += [{axis: plus(at, 1)}, {axis: plus(at, 3)}]
-    greet(peers + others)
 
     sent = []
     flow = {}
@@ -423,166 +362,302 @@
             m1 / first_fix / (jnp.sqrt(m2 / second_fix) + 1e-08)
         ).astype(both.dtype)
         own = both.at[rows(zl * n, n), cols(k)]
-        send((k, "d"), own, own, d_s.at[k], d_r.at[k], dp_2=1 - zl)
+        if not crossing(k):
+            send((k, "d"), own, own, d_s.at[k], d_r.at[k], dp_2=1 - zl)
+
+    def crossing(k):
+        return chunks[k][3]
 
     def line(k):
         if chunks[k][2] == 0:
             return "dp_1", "dp_0", x, y, 1, 4
         return "dp_0", "dp_1", y, x, 4, 1
 
-    def region(k, p1, p2, start, size):
+    def deep(k):
+        return n if crossing(k) else 2 * n
+
+    def region(k, p1, p2, start, size, z=zl):
         f1, f2 = line(k)[4:]
-        return full.at[rows((p1 * f1 + p2 * f2) * 2 * n + start, size, n), cols(k)]
+        if crossing(k):
+            start = start + z * n
+        return full.at[rows((p1 * f1 + p2 * f2) * 2 * n + start, size, n // 2), cols(k)]
+
+    def whole(k, p1, p2, z=zl):
+        return region(k, p1, p2, 0, deep(k), z)
+
+    def side(k, p1, p2, half):
+        size = deep(k) // 2
+        return region(k, p1, p2, half * size, size)
 
     def pass_on(k, i, axis, to, where, src=None):
         send((k, "a", i), where if src is None else src, where, ag_s.at[k, i], ag_r.at[k, i], **{axis: to})
 
+    def cross(k, d1, d2, src=None):
+        if crossing(k):
+            at1, at2 = line(k)[2:4]
+            where, i = whole(k, plus(at1, d1), plus(at2, d2)), 20 + d1 * 4 + d2
+            send((k, "a", i), where if src is None else src, where, ag_s.at[k, i], ag_r.at[k, i], dp_2=1 - zl)
+
     def ag_own(k):
         first, second, at1, at2 = line(k)[:4]
-        landed(both.at[rows((1 - zl) * n, n), cols(k)], d_r.at[k])
-        src, here = both.at[:, cols(k)], region(k, at1, at2, 0, 2 * n)
+        if crossing(k):
+            src = both.at[rows(zl * n, n), cols(k)]
+        else:
+            landed(both.at[rows((1 - zl) * n, n), cols(k)], d_r.at[k])
+            src = both.at[:, cols(k)]
+        here = whole(k, at1, at2)
         pass_on(k, 0, first, plus(at1, 1), here, src)
         pass_on(k, 1, first, plus(at1, 3), here, src)
         pass_on(k, 4, second, plus(at2, 1), here, src)
         pass_on(k, 8, second, plus(at2, 3), here, src)
+        cross(k, 0, 0, src)
         pltpu.make_async_copy(src, here, put_sem.at[k]).start()
 
     def ag_first(k):
         first, second, at1, at2 = line(k)[:4]
-        for j, d, to, half in ((0, 3, 1, 0), (1, 1, 3, 1)):
-            landed(region(k, plus(at1, d), at2, 0, 2 * n), ag_r.at[k, j])
-            pass_on(k, 2 + j, first, plus(at1, to), region(k, plus(at1, d), at2, half * n, n))
-            here = region(k, plus(at1, d), at2, 0, 2 * n)
+        for j, d, to in ((0, 3, 1), (1, 1, 3)):
+            here = whole(k, plus(at1, d), at2)
+            landed(here, ag_r.at[k, j])
+            pass_on(k, 2 + j, first, plus(at1, to), side(k, plus(at1, d), at2, j))
             pass_on(k, 5 + j, second, plus(at2, 1), here)
             pass_on(k, 9 + j, second, plus(at2, 3), here)
+            cross(k, d, 0)
 
     def ag_far(k):
         first, second, at1, at2 = line(k)[:4]
-        landed(region(k, plus(at1, 2), at2, 0, n), ag_r.at[k, 2])
-        landed(region(k, plus(at1, 2), at2, n, n), ag_r.at[k, 3])
-        here = region(k, plus(at1, 2), at2, 0, 2 * n)
+        landed(side(k, plus(at1, 2), at2, 0), ag_r.at[k, 2])
+        landed(side(k, plus(at1, 2), at2, 1), ag_r.at[k, 3])
+        here = whole(k, plus(at1, 2), at2)
         pass_on(k, 7, second, plus(at2, 1), here)
         pass_on(k, 11, second, plus(at2, 3), here)
+        cross(k, 2, 0)
 
     def ag_second(k, i):
         first, second, at1, at2 = line(k)[:4]
         d = (0, 3, 1, 2)[i]
-        landed(region(k, plus(at1, d), plus(at2, 3), 0, 2 * n), ag_r.at[k, 4 + i])
-        pass_on(k, 12 + i, second, plus(at2, 1), region(k, plus(at1, d), plus(at2, 3), 0, n))
-        landed(region(k, plus(at1, d), plus(at2, 1), 0, 2 * n), ag_r.at[k, 8 + i])
-        pass_on(k, 16 + i, second, plus(at2, 3), region(k, plus(at1, d), plus(at2, 1), n, n))
-
-    def ag_last(k):
+        landed(whole(k, plus(at1, d), plus(at2, 3)), ag_r.at[k, 4 + i])
+        pass_on(k, 12 + i, second, plus(at2, 1), side(k, plus(at1, d), plus(at2, 3), 0))
+        cross(k, d, 3)
+        landed(whole(k, plus(at1, d), plus(at2, 1)), ag_r.at[k, 8 + i])
+        pass_on(k, 16 + i, second, plus(at2, 3), side(k, plus(at1, d), plus(at2, 1), 1))
+        cross(k, d, 1)
+
+    def ag_last(k, i):
         first, second, at1, at2 = line(k)[:4]
-        for i, d in enumerate((0, 3, 1, 2)):
-            landed(region(k, plus(at1, d), plus(at2, 2), 0, n), ag_r.at[k, 12 + i])
-            landed(region(k, plus(at1, d), plus(at2, 2), n, n), ag_r.at[k, 16 + i])
-        landed(region(k, at1, at2, 0, 2 * n), put_sem.at[k])
-
-    def own_rows():
+        d = (0, 3, 1, 2)[i]
+        landed(side(k, plus(at1, d), plus(at2, 2), 0), ag_r.at[k, 12 + i])
+        landed(side(k, plus(at1, d), plus(at2, 2), 1), ag_r.at[k, 16 + i])
+        cross(k, d, 2)
+
+    def ag_end(k):
+        first, second, at1, at2 = line(k)[:4]
+        if crossing(k):
+            for d1 in range(4):
+                for d2 in range(4):
+                    landed(whole(k, plus(at1, d1), plus(at2, d2), 1 - zl), ag_r.at[k, 20 + d1 * 4 + d2])
+        landed(whole(k, at1, at2), put_sem.at[k])
+
+    above, below, beyond = plus(h, 1), plus(h, 3), plus(h, 2)
+    tall = proj.shape[0] // 2
+
+    def strip(of, who=c):
+        return prow.at[:, rows((of * 2 + who) * lanes, lanes)]
+
+    def bit(of, p):
+        return prow.at[pl.ds(p * tall, tall), rows((of * 2 + c) * lanes, lanes)]
+
+    def to_core(i, of, src=None):
+        send(("p", i), strip(of) if src is None else src, strip(of), p_s.at[i], p_r.at[i], mp_1=1 - c)
+
+    def rows_own():
         take.wait()
         keep.start()
-        for i, who in enumerate(others):
-            send(("p", i), stage, here, p_s.at[i], p_r.at[i], **who)
-
-    state = [
-        pltpu.make_async_copy(first_in, first_m, loc_sem.at[2]),
-        pltpu.make_async_copy(second_in, second_m, loc_sem.at[3]),
-    ]
-    for cp in state:
-        cp.start()
-    take = pltpu.make_async_copy(proj, stage, loc_sem.at[0])
-    take.start()
-    here = prow.at[:, rows((h * 2 + c) * lanes, lanes)]
-    keep = pltpu.make_async_copy(stage, here, loc_sem.at[1])
-
+        send(("p", 0), stage, strip(h), p_s.at[0], p_r.at[0], mp_0=above)
+        send(("p", 1), stage, strip(h), p_s.at[1], p_r.at[1], mp_0=below)
+        to_core(4, h, stage)
+
+    def rows_on():
+        landed(strip(below), p_r.at[0])
+        send(("p", 2), bit(below, 0), bit(below, 0), p_s.at[2], p_r.at[2], mp_0=above)
+        landed(strip(above), p_r.at[1])
+        send(("p", 3), bit(above, 1), bit(above, 1), p_s.at[3], p_r.at[3], mp_0=below)
+        to_core(5, below)
+        to_core(6, above)
+
+    def rows_far():
+        landed(bit(beyond, 0), p_r.at[2])
+        landed(bit(beyond, 1), p_r.at[3])
+        to_core(7, beyond)
+
+    def rows_end():
+        for i, of in enumerate((h, below, above, beyond)):
+            landed(strip(of, 1 - c), p_r.at[4 + i])
+        keep.wait()
+
+    take, *state = early
+    keep = pltpu.make_async_copy(stage, strip(h), keep_sem)
+
+    def dots(k):
+        part[:, cols(k)] = lax.dot_general(
+            pa[...], ga[:, cols(k)], (((0,), (0,)), ((), ())), preferred_element_type=f32
+        ).astype(part.dtype)
+
+    dots(0)
     rs_far(0)
     rs_near(0)
+    dots(1)
     rs_far(1)
     rs_turn(0)
     rs_near(1)
+    dots(2)
     rs_far(2)
+    rows_own()
     rs_sum(0)
     rs_turn(1)
     rs_near(2)
+    dots(3)
+    rs_far(3)
     for cp in state:
         cp.wait()
     adam(0)
+    ag_own(0)
     rs_sum(1)
     rs_turn(2)
-    ag_own(0)
+    rs_near(3)
     adam(1)
+    ag_own(1)
+    ag_first(0)
     rs_sum(2)
-    ag_own(1)
+    rs_turn(3)
+    ag_far(0)
     adam(2)
-    ag_first(0)
+    rs_sum(3)
+    ag_first(1)
     ag_own(2)
-    own_rows()
-    ag_first(1)
-    ag_far(0)
+    rows_on()
+    adam(3)
+    ag_second(0, 0)
+    ag_far(1)
+    ag_own(3)
+    ag_second(0, 1)
     ag_first(2)
-    ag_far(1)
+    ag_second(0, 2)
+    ag_second(0, 3)
+    ag_first(3)
+    for i in range(4):
+        ag_last(0, i)
+    rows_far()
     ag_far(2)
+    ag_far(3)
     for i in range(4):
-        for k in range(3):
+        for k in (1, 2, 3):
             ag_second(k, i)
-    for k in range(3):
-        ag_last(k)
-    for i, who in enumerate(others):
-        frm = plus(h, 4 - (i + 1) // 2) * 2 + lax.rem(c + (i + 1) % 2, 2)
-        landed(prow.at[:, rows(frm * lanes, lanes)], p_r.at[i])
-    keep.wait()
+    for i in range(4):
+        for k in (1, 2, 3):
+            ag_last(k, i)
+    for k in range(4):
+        ag_end(k)
+    rows_end()
     for cp in sent:
         cp.wait_send()
 
 
 def split(cols):
-    third = cols // 384 * 128
-    return ((0, third, 0), (third, third, 0), (2 * third, cols - 2 * third, 1))
-
-
-def update(part, first_moment, second_moment, projector):
+    tiles = cols // 128
+    first, second, third = tiles * 4 // 26, tiles * 6 // 26, tiles * 8 // 26
+    ends = (0, first, first + second, first + second + third, tiles)
+    kinds = ((0, True), (0, True), (0, False), (1, False))
+    return tuple((128 * a, 128 * (b - a), *kind) for a, b, kind in zip(ends, ends[1:], kinds))
+
+
+def step_kernel(
+    chunks, inp, proj, grads, first_in, second_in, new_first, new_second, full, prow,
+    pa, ga, part, stage, first_m, second_m, early_sem, *rest
+):
+    y, x, zl, h, c = place()
+    peers = [{"mp_1": 1 - c}, {"dp_2": 1 - zl}]
+    for axis, at in (("dp_0", y), ("dp_1", x), ("mp_0", h)):
+        peers += [{axis: lax.rem(at + 1, 4)}, {axis: lax.rem(at + 3, 4)}]
+    peers.append({"dp_0": h, "mp_0": y, "mp_1": 1 - c})
+    early = [
+        pltpu.make_async_copy(src, dst, early_sem.at[i])
+        for i, (src, dst) in enumerate(((proj, stage), (first_in, first_m), (second_in, second_m)))
+    ]
+    for cp in early:
+        cp.start()
+    greet(peers, ({"dp_0": h, "mp_0": y}, y != h))
+    bufs1, rest = rest[:13], rest[13:]
+    sems1, rest = rest[:15], rest[15:]
+    bufs2, sems2 = rest[:11], rest[11:]
+    finish = projected_body(inp, proj, grads, pa, ga, *bufs1, *sems1)
+    update_body(
+        chunks, early, pa, ga, proj, new_first, new_second, full, prow,
+        part, *bufs2, stage, first_m, second_m, *sems2,
+    )
+    finish()
+
+
+def step(inputs, projector, out_grads, first_moment, second_moment):
+    tok, feats = inputs.shape
+    feat, lanes = projector.shape
     n, cols = first_moment.shape
-    feat, lanes = projector.shape
     bf, f32 = jnp.bfloat16, jnp.float32
+    small = pltpu.VMEM((2, tok // 4, lanes), f32)
+    slot = pltpu.VMEM((n, cols), bf)
     chunks = split(cols)
-    slot = pltpu.VMEM((n, cols), bf)
     count = len(chunks)
     return pl.pallas_call(
-        functools.partial(update_kernel, chunks),
-        name="update",
+        functools.partial(step_kernel, chunks),
+        name="step",
         out_shape=(
             jax.ShapeDtypeStruct((n, cols), f32),
             jax.ShapeDtypeStruct((n, cols), f32),
             jax.ShapeDtypeStruct((32 * n, cols), bf),
             jax.ShapeDtypeStruct((feat, 8 * lanes), bf),
         ),
-        in_specs=[VMEM, ANY, ANY, ANY],
+        in_specs=[ANY] * 5,
         out_specs=(VMEM, VMEM, ANY, ANY),
-        scratch_shapes=[slot] * 10 + [
-            pltpu.VMEM((2 * n, cols), bf),
+        scratch_shapes=[
+            pltpu.VMEM((4 * tok, 2 * lanes), bf),
+            pltpu.VMEM((4 * tok, cols), bf),
+            pltpu.VMEM((8 * n, cols), bf),
             pltpu.VMEM((feat, lanes), bf),
             pltpu.VMEM((n, cols), f32),
             pltpu.VMEM((n, cols), f32),
-            DMA((4,)),
+            DMA((3,)),
+            pltpu.VMEM((2, 2 * tok, feats), bf),
+            pltpu.VMEM((4 * feat, 2 * lanes), bf),
+            pltpu.VMEM((2, 2 * tok, lanes), f32),
+            pltpu.VMEM((2, 2 * tok, lanes), f32),
+            pltpu.VMEM((2, 2 * tok, lanes), f32),
+            *[small] * 8,
+            DMA((2,)),
+            DMA((6,)), DMA((6,)),
+            DMA((6,)), DMA((6,)),
+            DMA((1,)), DMA((8,)),
+            DMA((8, 3)), DMA((8, 2)),
+            DMA((2,)), DMA((2,)),
+            DMA((2, 6)), DMA((2, 6)),
+            DMA((2, 8)), DMA((2, 8)),
+            *[slot] * 10,
+            pltpu.VMEM((2 * n, cols), bf),
+            DMA,
             DMA((count,)),
             DMA((count, 7)), DMA((count, 7)),
             DMA((count,)), DMA((count,)),
-            DMA((count, 20)), DMA((count, 20)),
-            DMA((7,)), DMA((7,)),
+            DMA((count, 36)), DMA((count, 36)),
+            DMA((8,)), DMA((8,)),
         ],
         compiler_params=pltpu.CompilerParams(
-            collective_id=1, has_side_effects=True, vmem_limit_bytes=16 << 20
+            collective_id=0, has_side_effects=True, vmem_limit_bytes=24 << 20
         ),
-    )(part, *(in_hbm(v) for v in (first_moment, second_moment, projector)))
+    )(*(in_hbm(v) for v in (inputs, projector, out_grads, first_moment, second_moment)))
 
 
 def per_device(inputs, projector, out_grads, weights, first_moment, second_moment):
-    projected, grads = gather_projected(inputs, projector, out_grads)
-    part = lax.dot_general(
-        projected, grads, (((0,), (0,)), ((), ())), preferred_element_type=jnp.float32
-    ).astype(jnp.bfloat16)
-    new_first, new_second, full, ranks = update(part, first_moment, second_moment, projector)
+    new_first, new_second, full, ranks = step(
+        inputs, projector, out_grads, first_moment, second_moment
+    )
     lifted = jnp.dot(ranks, full, preferred_element_type=jnp.float32)
     new_weights = (weights.astype(jnp.float32) - 2.0 * lifted).astype(jnp.bfloat16)
     return (new_weights, new_first, new_second)

time: 130 us -> 128 us (0.985)
  Pallas kernels: 121 us -> 119 us
    pallas_call x2 -> x1, Pallas kernels: 121 us -> 119 us  [step(): pl.pallas_call(functools.partial(step_kernel, chunks), name='step', out_s...]
    dot_general x1, matrix products: 5.16 us -> 6.52 us  [per_device(): lifted = jnp.dot(ranks, full, preferred_element_type=jnp.float32)]
where the time goes in v4:
time: 128 us
  Pallas kernels  119 us (93%)
  matrix products  6.52 us (5%)
  local copies, waits for them, and re-layouts  1.51 us (1%)
    pallas_call x1, Pallas kernels, step(): pl.pallas_call(functools.partial(step_kernel, chunks), name='step', out_s...  119 us
    dot_general x1, matrix products, per_device(): lifted = jnp.dot(ranks, full, preferred_element_type=jnp.float32)  6.52 us

profile of v4, /device:TPU:4, one launch (start us, length us, event | category | flops | bytes accessed | tf_op | source)
XLA Modules:
  0.0 127.6 jit_solution(12589913722043948464)
XLA Ops:
  0.6 118.9 %step.1 = (f32[32,3328]{1,0:T(8,128)S(1)}, f32[32,3328]{1,0:T(8,128)S(1)}, bf16[1024,3328]{1,0:T(8,128)(2,1)S(1)}, bf16[512,1024]{1,0:T(8,128)(2,1)S(1)}) custom-call(bf16[128,2048]{1,0:T(8,128)(2,1)} %inp.1, bf16[512,128]{1,0:T(8,128)(2,1)} %proj.1, bf16[128,3328]{1,0:T(8,128)(2,1)} %grads.1, f32[32,3328]{1,0:T(8,128)} %first_in.1, f32[32,3328]{1,0:T(8,128)} %second_in.1), custom_call_target="tpu_custom_call" | custom-call | tf_op jit(solution)/shard_map/step/pallas_call | solution.py:609
  119.5 6.5 %subtract_convert_fusion = bf16[512,3328]{1,0:T(8,128)(2,1)} fusion(bf16[512,3328]{1,0:T(8,128)(2,1)} %param.9, bf16[512,1024]{1,0:T(8,128)(2,1)S(1)} %get-tuple-element.7, bf16[1024,3328]{1,0:T(8,128)(2,1)S(1)} %get-tuple-element.8), kind=kOutput, calls=%fused_computation | convolution fusion | flops 3496476672 | bytes 14680064 | tf_op jit(solution)/shard_map/dot_general | solution.py:661
  126.1 0.8 copy.11
  126.8 0.8 copy.12

commit v5 on v4

--- a/solution.py
+++ b/solution.py
@@ -16,6 +16,30 @@
 ANY = pl.BlockSpec(memory_space=pl.ANY)
 VMEM = pl.BlockSpec(memory_space=pltpu.VMEM)
 DMA = pltpu.SemaphoreType.DMA
+
+
+ORDER = (
+    ('dots', 0), ('far', 0), ('dots', 1), ('far', 1), ('dots', 2), ('far', 2), ('dots', 3), ('far', 3),
+    ('dots', 4), ('far', 4), ('near', 0), ('near', 1), ('near', 2), ('near', 3), ('near', 4), ('turn', 0),
+    ('turn', 1), ('turn', 2), ('turn', 3), ('turn', 4), ('sum', 0), ('sum', 1), ('sum', 2), ('adam', 0),
+    ('sum', 3), ('adam', 1), ('rows_on',), ('own', 1), ('sum', 4), ('adam', 2), ('own', 2), ('own', 0),
+    ('first', 1, 0), ('adam', 3), ('first', 1, 1), ('second', 1, 0, 0), ('second', 1, 0, 1), ('first', 2, 0),
+    ('first', 2, 1), ('second', 2, 0, 0), ('second', 2, 0, 1), ('adam', 4), ('first', 0, 0), ('first', 0, 1),
+    ('second', 0, 0, 0), ('second', 0, 0, 1), ('farg', 1), ('rows_far',), ('second', 1, 1, 0),
+    ('second', 1, 1, 1), ('second', 1, 2, 0), ('second', 1, 2, 1), ('last', 1, 0), ('farg', 2), ('own', 3),
+    ('second', 2, 1, 0), ('second', 2, 1, 1), ('second', 0, 1, 0), ('second', 0, 1, 1), ('second', 2, 2, 0),
+    ('second', 2, 2, 1), ('last', 2, 0), ('second', 0, 2, 0), ('farg', 0), ('second', 0, 2, 1),
+    ('last', 0, 0), ('second', 1, 3, 0), ('second', 1, 3, 1), ('last', 1, 1), ('last', 1, 2),
+    ('second', 2, 3, 0), ('second', 2, 3, 1), ('second', 3, 0, 0), ('second', 3, 0, 1), ('last', 0, 1),
+    ('second', 0, 3, 1), ('own', 4), ('first', 3, 0), ('second', 0, 3, 0), ('last', 0, 2), ('first', 3, 1),
+    ('last', 2, 1), ('last', 2, 2), ('last', 1, 3), ('last', 3, 0), ('last', 2, 3), ('first', 4, 0),
+    ('second', 4, 0, 0), ('first', 4, 1), ('second', 4, 0, 1), ('farg', 3), ('second', 3, 1, 0),
+    ('second', 3, 1, 1), ('last', 0, 3), ('end', 0), ('second', 4, 1, 0), ('second', 4, 1, 1),
+    ('second', 3, 2, 1), ('second', 3, 2, 0), ('second', 4, 2, 1), ('farg', 4), ('second', 4, 2, 0),
+    ('last', 4, 0), ('last', 4, 1), ('second', 3, 3, 1), ('second', 3, 3, 0), ('second', 4, 3, 0),
+    ('last', 3, 1), ('second', 4, 3, 1), ('end', 1), ('last', 4, 2), ('last', 3, 2), ('end', 2),
+    ('last', 3, 3), ('end', 3), ('last', 4, 3), ('end', 4), ('rows_end',),
+)
 
 
 def in_hbm(x):
@@ -64,7 +88,7 @@
 def projected_body(
     inp, proj, grads, pa, ga,
     inp4, pq, own, out_half, half_in, via_d, via_u, raw_d, raw_u, turn_u, turn_d, add_d, add_u,
-    loc_sem, in_s, in_r, g_s, g_r, sw_s, pq_r, ring_s, ring_r, half_s, half_r, rs_s, rs_r, sh_s, sh_r,
+    rows_own, loc_sem, in_s, in_r, g_s, g_r, sw_s, pq_r, ring_s, ring_r, half_s, half_r, rs_s, rs_r, sh_s, sh_r,
 ):
     y, x, zl, h, c = place()
     up, down = lax.rem(y + 1, 4), lax.rem(y + 3, 4)
@@ -252,6 +276,7 @@
         landed(share(k, beyond, 0, q), sh_r.at[k, 2])
         landed(share(k, beyond, q, q), sh_r.at[k, 3])
         send(share(k, beyond), share(k, beyond), sh_s.at[k, 7], sh_r.at[k, 7], mp_1=1 - c)
+    rows_own()
     for k in range(2):
         for i, of in enumerate((h, below, above, beyond)):
             landed(share(k, of, who=1 - c), sh_r.at[k, 4 + i])
@@ -413,15 +438,15 @@
         cross(k, 0, 0, src)
         pltpu.make_async_copy(src, here, put_sem.at[k]).start()
 
-    def ag_first(k):
+    def ag_first(k, j):
         first, second, at1, at2 = line(k)[:4]
-        for j, d, to in ((0, 3, 1), (1, 1, 3)):
-            here = whole(k, plus(at1, d), at2)
-            landed(here, ag_r.at[k, j])
-            pass_on(k, 2 + j, first, plus(at1, to), side(k, plus(at1, d), at2, j))
-            pass_on(k, 5 + j, second, plus(at2, 1), here)
-            pass_on(k, 9 + j, second, plus(at2, 3), here)
-            cross(k, d, 0)
+        d, to = ((3, 1), (1, 3))[j]
+        here = whole(k, plus(at1, d), at2)
+        landed(here, ag_r.at[k, j])
+        pass_on(k, 2 + j, first, plus(at1, to), side(k, plus(at1, d), at2, j))
+        pass_on(k, 5 + j, second, plus(at2, 1), here)
+        pass_on(k, 9 + j, second, plus(at2, 3), here)
+        cross(k, d, 0)
 
     def ag_far(k):
         first, second, at1, at2 = line(k)[:4]
@@ -432,15 +457,13 @@
         pass_on(k, 11, second, plus(at2, 3), here)
         cross(k, 2, 0)
 
-    def ag_second(k, i):
+    def ag_second(k, i, j):
         first, second, at1, at2 = line(k)[:4]
         d = (0, 3, 1, 2)[i]
-        landed(whole(k, plus(at1, d), plus(at2, 3)), ag_r.at[k, 4 + i])
-        pass_on(k, 12 + i, second, plus(at2, 1), side(k, plus(at1, d), plus(at2, 3), 0))
-        cross(k, d, 3)
-        landed(whole(k, plus(at1, d), plus(at2, 1)), ag_r.at[k, 8 + i])
-        pass_on(k, 16 + i, second, plus(at2, 3), side(k, plus(at1, d), plus(at2, 1), 1))
-        cross(k, d, 1)
+        frm, to = ((3, 1), (1, 3))[j]
+        landed(whole(k, plus(at1, d), plus(at2, frm)), ag_r.at[k, 4 + i + 4 * j])
+        pass_on(k, 12 + i + 4 * j, second, plus(at2, to), side(k, plus(at1, d), plus(at2, frm), j))
+        cross(k, d, frm)
 
     def ag_last(k, i):
         first, second, at1, at2 = line(k)[:4]
@@ -469,14 +492,9 @@
     def to_core(i, of, src=None):
         send(("p", i), strip(of) if src is None else src, strip(of), p_s.at[i], p_r.at[i], mp_1=1 - c)
 
-    def rows_own():
+    def rows_on():
         take.wait()
         keep.start()
-        send(("p", 0), stage, strip(h), p_s.at[0], p_r.at[0], mp_0=above)
-        send(("p", 1), stage, strip(h), p_s.at[1], p_r.at[1], mp_0=below)
-        to_core(4, h, stage)
-
-    def rows_on():
         landed(strip(below), p_r.at[0])
         send(("p", 2), bit(below, 0), bit(below, 0), p_s.at[2], p_r.at[2], mp_0=above)
         landed(strip(above), p_r.at[1])
@@ -502,76 +520,29 @@
             pa[...], ga[:, cols(k)], (((0,), (0,)), ((), ())), preferred_element_type=f32
         ).astype(part.dtype)
 
-    dots(0)
-    rs_far(0)
-    rs_near(0)
-    dots(1)
-    rs_far(1)
-    rs_turn(0)
-    rs_near(1)
-    dots(2)
-    rs_far(2)
-    rows_own()
-    rs_sum(0)
-    rs_turn(1)
-    rs_near(2)
-    dots(3)
-    rs_far(3)
     for cp in state:
         cp.wait()
-    adam(0)
-    ag_own(0)
-    rs_sum(1)
-    rs_turn(2)
-    rs_near(3)
-    adam(1)
-    ag_own(1)
-    ag_first(0)
-    rs_sum(2)
-    rs_turn(3)
-    ag_far(0)
-    adam(2)
-    rs_sum(3)
-    ag_first(1)
-    ag_own(2)
-    rows_on()
-    adam(3)
-    ag_second(0, 0)
-    ag_far(1)
-    ag_own(3)
-    ag_second(0, 1)
-    ag_first(2)
-    ag_second(0, 2)
-    ag_second(0, 3)
-    ag_first(3)
-    for i in range(4):
-        ag_last(0, i)
-    rows_far()
-    ag_far(2)
-    ag_far(3)
-    for i in range(4):
-        for k in (1, 2, 3):
-            ag_second(k, i)
-    for i in range(4):
-        for k in (1, 2, 3):
-            ag_last(k, i)
-    for k in range(4):
-        ag_end(k)
-    rows_end()
+    steps = {
+        "dots": dots, "far": rs_far, "near": rs_near, "turn": rs_turn, "sum": rs_sum, "adam": adam,
+        "own": ag_own, "first": ag_first, "farg": ag_far, "second": ag_second, "last": ag_last, "end": ag_end,
+        "rows_on": rows_on, "rows_far": rows_far, "rows_end": rows_end,
+    }
+    for what, *which in ORDER:
+        steps[what](*which)
     for cp in sent:
         cp.wait_send()
 
 
 def split(cols):
     tiles = cols // 128
-    first, second, third = tiles * 4 // 26, tiles * 6 // 26, tiles * 8 // 26
-    ends = (0, first, first + second, first + second + third, tiles)
-    kinds = ((0, True), (0, True), (0, False), (1, False))
+    widths = [tiles * part // 26 for part in (3, 4, 5, 8)]
+    ends = [sum(widths[:k]) for k in range(5)] + [tiles]
+    kinds = ((0, False), (1, True), (1, True), (0, False), (1, False))
     return tuple((128 * a, 128 * (b - a), *kind) for a, b, kind in zip(ends, ends[1:], kinds))
 
 
 def step_kernel(
-    chunks, inp, proj, grads, first_in, second_in, new_first, new_second, full, prow,
+    chunks, inp, proj, grads, first_in, second_in, weights, new_first, new_second, full, prow, near,
     pa, ga, part, stage, first_m, second_m, early_sem, *rest
 ):
     y, x, zl, h, c = place()
@@ -581,7 +552,7 @@
     peers.append({"dp_0": h, "mp_0": y, "mp_1": 1 - c})
     early = [
         pltpu.make_async_copy(src, dst, early_sem.at[i])
-        for i, (src, dst) in enumerate(((proj, stage), (first_in, first_m), (second_in, second_m)))
+        for i, (src, dst) in enumerate(((proj, stage), (first_in, first_m), (second_in, second_m), (weights, near)))
     ]
     for cp in early:
         cp.start()
@@ -589,15 +560,32 @@
     bufs1, rest = rest[:13], rest[13:]
     sems1, rest = rest[:15], rest[15:]
     bufs2, sems2 = rest[:11], rest[11:]
-    finish = projected_body(inp, proj, grads, pa, ga, *bufs1, *sems1)
+    p_s, p_r = sems2[-2:]
+    lanes = proj.shape[1]
+    mine = prow.at[:, rows((h * 2 + c) * lanes, lanes)]
+    given = [
+        remote(proj, mine, p_s.at[i], p_r.at[i], **where)
+        for i, where in (
+            (0, {"mp_0": lax.rem(h + 1, 4)}), (1, {"mp_0": lax.rem(h + 3, 4)}), (4, {"mp_1": 1 - c})
+        )
+    ]
+
+    def rows_own():
+        for cp in given:
+            cp.start()
+
+    finish = projected_body(inp, proj, grads, pa, ga, *bufs1, rows_own, *sems1)
     update_body(
-        chunks, early, pa, ga, proj, new_first, new_second, full, prow,
+        chunks, early[:3], pa, ga, proj, new_first, new_second, full, prow,
         part, *bufs2, stage, first_m, second_m, *sems2,
     )
     finish()
-
-
-def step(inputs, projector, out_grads, first_moment, second_moment):
+    for cp in given:
+        cp.wait_send()
+    early[3].wait()
+
+
+def step(inputs, projector, out_grads, first_moment, second_moment, weights):
     tok, feats = inputs.shape
     feat, lanes = projector.shape
     n, cols = first_moment.shape
@@ -614,9 +602,10 @@
             jax.ShapeDtypeStruct((n, cols), f32),
             jax.ShapeDtypeStruct((32 * n, cols), bf),
             jax.ShapeDtypeStruct((feat, 8 * lanes), bf),
+            jax.ShapeDtypeStruct(weights.shape, weights.dtype),
         ),
-        in_specs=[ANY] * 5,
-        out_specs=(VMEM, VMEM, ANY, ANY),
+        in_specs=[ANY] * 6,
+        out_specs=(VMEM, VMEM, ANY, ANY, ANY),
         scratch_shapes=[
             pltpu.VMEM((4 * tok, 2 * lanes), bf),
             pltpu.VMEM((4 * tok, cols), bf),
@@ -624,7 +613,7 @@
             pltpu.VMEM((feat, lanes), bf),
             pltpu.VMEM((n, cols), f32),
             pltpu.VMEM((n, cols), f32),
-            DMA((3,)),
+            DMA((4,)),
             pltpu.VMEM((2, 2 * tok, feats), bf),
             pltpu.VMEM((4 * feat, 2 * lanes), bf),
             pltpu.VMEM((2, 2 * tok, lanes), f32),
@@ -651,12 +640,12 @@
         compiler_params=pltpu.CompilerParams(
             collective_id=0, has_side_effects=True, vmem_limit_bytes=24 << 20
         ),
-    )(*(in_hbm(v) for v in (inputs, projector, out_grads, first_moment, second_moment)))
+    )(*(in_hbm(v) for v in (inputs, projector, out_grads, first_moment, second_moment, weights)))
 
 
 def per_device(inputs, projector, out_grads, weights, first_moment, second_moment):
-    new_first, new_second, full, ranks = step(
-        inputs, projector, out_grads, first_moment, second_moment
+    new_first, new_second, full, ranks, weights = step(
+        inputs, projector, out_grads, first_moment, second_moment, weights
     )
     lifted = jnp.dot(ranks, full, preferred_element_type=jnp.float32)
     new_weights = (weights.astype(jnp.float32) - 2.0 * lifted).astype(jnp.bfloat16)

time: 128 us -> 124 us (0.969)
  Pallas kernels: 119 us -> 116 us
  matrix products: 6.52 us -> 5.08 us
    pallas_call x1, Pallas kernels: 119 us -> 116 us  [step(): pl.pallas_call(functools.partial(step_kernel, chunks), name='step', out_s...]
    dot_general x1, matrix products: 6.52 us -> 5.08 us  [per_device(): lifted = jnp.dot(ranks, full, preferred_element_type=jnp.float32)]
where the time goes in v5:
time: 124 us
  Pallas kernels  116 us (94%)
  matrix products  5.08 us (4%)
  local copies, waits for them, and re-layouts  1.51 us (1%)
    pallas_call x1, Pallas kernels, step(): pl.pallas_call(functools.partial(step_kernel, chunks), name='step', out_s...  116 us
    dot_general x1, matrix products, per_device(): lifted = jnp.dot(ranks, full, preferred_element_type=jnp.float32)  5.08 us

profile of v5, /device:TPU:4, one launch (start us, length us, event | category | flops | bytes accessed | tf_op | source)
XLA Modules:
  0.0 123.7 jit_solution(17663048791309937961)
XLA Ops:
  0.6 116.5 %step.1 = (f32[32,3328]{1,0:T(8,128)S(1)}, f32[32,3328]{1,0:T(8,128)S(1)}, bf16[1024,3328]{1,0:T(8,128)(2,1)S(1)}, bf16[512,1024]{1,0:T(8,128)(2,1)S(1)}, bf16[512,3328]{1,0:T(8,128)(2,1)S(1)}) custom-call(bf16[128,2048]{1,0:T(8,128)(2,1)} %inp.1, bf16[512,128]{1,0:T(8,128)(2,1)} %proj.1, bf16[128,3328]{1,0:T(8,128)(2,1)} %grads.1, f32[32,3328]{1,0:T(8,128)} %first_in.1, ...), custom_call_target="tpu_custom_call" | custom-call | tf_op jit(solution)/shard_map/step/pallas_call | solution.py:597
  117.1 5.1 %subtract_convert_fusion = bf16[512,3328]{1,0:T(8,128)(2,1)} fusion(bf16[512,3328]{1,0:T(8,128)(2,1)S(1)} %get-tuple-element.8, bf16[512,1024]{1,0:T(8,128)(2,1)S(1)} %get-tuple-element.9, bf16[1024,3328]{1,0:T(8,128)(2,1)S(1)} %get-tuple-element.10), kind=kOutput, calls=%fused_computation | convolution fusion | flops 3496476672 | bytes 14680064 | tf_op jit(solution)/shard_map/dot_general | solution.py:650
  122.2 0.8 copy.11
  123.0 0.8 copy.12

commit v6 on v5

--- a/solution.py
+++ b/solution.py
@@ -20,25 +20,21 @@
 
 ORDER = (
     ('dots', 0), ('far', 0), ('dots', 1), ('far', 1), ('dots', 2), ('far', 2), ('dots', 3), ('far', 3),
-    ('dots', 4), ('far', 4), ('near', 0), ('near', 1), ('near', 2), ('near', 3), ('near', 4), ('turn', 0),
-    ('turn', 1), ('turn', 2), ('turn', 3), ('turn', 4), ('sum', 0), ('sum', 1), ('sum', 2), ('adam', 0),
-    ('sum', 3), ('adam', 1), ('rows_on',), ('own', 1), ('sum', 4), ('adam', 2), ('own', 2), ('own', 0),
-    ('first', 1, 0), ('adam', 3), ('first', 1, 1), ('second', 1, 0, 0), ('second', 1, 0, 1), ('first', 2, 0),
-    ('first', 2, 1), ('second', 2, 0, 0), ('second', 2, 0, 1), ('adam', 4), ('first', 0, 0), ('first', 0, 1),
-    ('second', 0, 0, 0), ('second', 0, 0, 1), ('farg', 1), ('rows_far',), ('second', 1, 1, 0),
-    ('second', 1, 1, 1), ('second', 1, 2, 0), ('second', 1, 2, 1), ('last', 1, 0), ('farg', 2), ('own', 3),
-    ('second', 2, 1, 0), ('second', 2, 1, 1), ('second', 0, 1, 0), ('second', 0, 1, 1), ('second', 2, 2, 0),
-    ('second', 2, 2, 1), ('last', 2, 0), ('second', 0, 2, 0), ('farg', 0), ('second', 0, 2, 1),
-    ('last', 0, 0), ('second', 1, 3, 0), ('second', 1, 3, 1), ('last', 1, 1), ('last', 1, 2),
-    ('second', 2, 3, 0), ('second', 2, 3, 1), ('second', 3, 0, 0), ('second', 3, 0, 1), ('last', 0, 1),
-    ('second', 0, 3, 1), ('own', 4), ('first', 3, 0), ('second', 0, 3, 0), ('last', 0, 2), ('first', 3, 1),
-    ('last', 2, 1), ('last', 2, 2), ('last', 1, 3), ('last', 3, 0), ('last', 2, 3), ('first', 4, 0),
-    ('second', 4, 0, 0), ('first', 4, 1), ('second', 4, 0, 1), ('farg', 3), ('second', 3, 1, 0),
-    ('second', 3, 1, 1), ('last', 0, 3), ('end', 0), ('second', 4, 1, 0), ('second', 4, 1, 1),
-    ('second', 3, 2, 1), ('second', 3, 2, 0), ('second', 4, 2, 1), ('farg', 4), ('second', 4, 2, 0),
-    ('last', 4, 0), ('last', 4, 1), ('second', 3, 3, 1), ('second', 3, 3, 0), ('second', 4, 3, 0),
-    ('last', 3, 1), ('second', 4, 3, 1), ('end', 1), ('last', 4, 2), ('last', 3, 2), ('end', 2),
-    ('last', 3, 3), ('end', 3), ('last', 4, 3), ('end', 4), ('rows_end',),
+    ('near', 0), ('near', 1), ('near', 2), ('near', 3), ('turn', 0), ('turn', 1), ('turn', 2), ('turn', 3),
+    ('sum', 0), ('sum', 1), ('sum', 2), ('adam', 0), ('sum', 3), ('adam', 1), ('rows_on',), ('own', 1),
+    ('adam', 2), ('own', 0), ('adam', 3), ('first', 1, 0), ('first', 1, 1), ('second', 1, 0, 0),
+    ('second', 1, 0, 1), ('own', 2), ('first', 0, 0), ('own', 3), ('first', 0, 1), ('second', 0, 0, 0),
+    ('second', 0, 0, 1), ('farg', 1), ('rows_far',), ('second', 1, 1, 0), ('second', 1, 1, 1),
+    ('second', 2, 0, 0), ('second', 1, 2, 0), ('second', 1, 2, 1), ('second', 2, 0, 1), ('last', 1, 0),
+    ('second', 0, 1, 0), ('second', 0, 1, 1), ('first', 2, 0), ('first', 2, 1), ('first', 3, 0),
+    ('first', 3, 1), ('second', 3, 0, 1), ('farg', 0), ('second', 3, 0, 0), ('second', 0, 2, 0),
+    ('second', 0, 2, 1), ('last', 0, 0), ('second', 1, 3, 0), ('second', 1, 3, 1), ('last', 1, 1),
+    ('last', 2, 0), ('last', 1, 2), ('last', 0, 1), ('farg', 2), ('second', 2, 1, 0), ('second', 2, 1, 1),
+    ('second', 3, 1, 0), ('second', 3, 1, 1), ('second', 2, 2, 0), ('second', 2, 2, 1), ('farg', 3),
+    ('second', 3, 2, 0), ('second', 3, 2, 1), ('last', 3, 0), ('last', 1, 3), ('second', 0, 3, 0),
+    ('second', 0, 3, 1), ('last', 3, 1), ('last', 0, 2), ('second', 2, 3, 0), ('second', 2, 3, 1),
+    ('second', 3, 3, 0), ('second', 3, 3, 1), ('last', 2, 1), ('last', 3, 2), ('last', 2, 2), ('end', 1),
+    ('last', 0, 3), ('end', 0), ('last', 3, 3), ('last', 2, 3), ('end', 2), ('end', 3), ('rows_end',),
 )
 
 
@@ -535,9 +531,9 @@
 
 def split(cols):
     tiles = cols // 128
-    widths = [tiles * part // 26 for part in (3, 4, 5, 8)]
-    ends = [sum(widths[:k]) for k in range(5)] + [tiles]
-    kinds = ((0, False), (1, True), (1, True), (0, False), (1, False))
+    widths = [tiles * part // 26 for part in (6, 9, 5)]
+    ends = [sum(widths[:k]) for k in range(4)] + [tiles]
+    kinds = ((0, False), (1, True), (0, False), (1, False))
     return tuple((128 * a, 128 * (b - a), *kind) for a, b, kind in zip(ends, ends[1:], kinds))
 
 

time: 124 us -> 123 us (level)
    pallas_call x1, Pallas kernels: 116 us -> 115 us  [step(): pl.pallas_call(functools.partial(step_kernel, chunks), name='step', out_s...]
where the time goes in v6:
time: 123 us; the launch traced here: 122 us
  Pallas kernels  115 us (93%)
  matrix products  5.09 us (4%)
  local copies, waits for them, and re-layouts  1.51 us (1%)
    pallas_call x1, Pallas kernels, step(): pl.pallas_call(functools.partial(step_kernel, chunks), name='step', out_s...  115 us
    dot_general x1, matrix products, per_device(): lifted = jnp.dot(ranks, full, preferred_element_type=jnp.float32)  5.09 us

profile of v6, /device:TPU:4, one launch (start us, length us, event | category | flops | bytes accessed | tf_op | source)
XLA Modules:
  0.0 122.4 jit_solution(13217282971102330533)
XLA Ops:
  0.6 115.2 %step.1 = (f32[32,3328]{1,0:T(8,128)S(1)}, f32[32,3328]{1,0:T(8,128)S(1)}, bf16[1024,3328]{1,0:T(8,128)(2,1)S(1)}, bf16[512,1024]{1,0:T(8,128)(2,1)S(1)}, bf16[512,3328]{1,0:T(8,128)(2,1)S(1)}) custom-call(bf16[128,2048]{1,0:T(8,128)(2,1)} %inp.1, bf16[512,128]{1,0:T(8,128)(2,1)} %proj.1, bf16[128,3328]{1,0:T(8,128)(2,1)} %grads.1, f32[32,3328]{1,0:T(8,128)} %first_in.1, ...), custom_call_target="tpu_custom_call" | custom-call | tf_op jit(solution)/shard_map/step/pallas_call | solution.py:593
  115.8 5.1 %subtract_convert_fusion = bf16[512,3328]{1,0:T(8,128)(2,1)} fusion(bf16[512,3328]{1,0:T(8,128)(2,1)S(1)} %get-tuple-element.8, bf16[512,1024]{1,0:T(8,128)(2,1)S(1)} %get-tuple-element.9, bf16[1024,3328]{1,0:T(8,128)(2,1)S(1)} %get-tuple-element.10), kind=kOutput, calls=%fused_computation | convolution fusion | flops 3496476672 | bytes 14680064 | tf_op jit(solution)/shard_map/dot_general | solution.py:646
  120.9 0.8 copy.11
  121.7 0.8 copy.12
